TPU v7x, 32 devices: a whole 2x2x4 slice. The times are simulated.
32 devices in a mesh: dp: 8 (over z, core), seq: 4 (over y, x).
Axes of the slice: x: 2, y: 2, z: 4, core: 2. Of those that a mesh axis runs over, the one named last changes fastest.
Arguments:
- hidden: bfloat16 [8, 2, 256, 8192], P('dp', None, 'seq'), may hold values from -6 to 6
- queries: bfloat16 [8, 2, 256, 4096], P('dp', None, 'seq'), may hold values from -240 to 240
- key_matrix: bfloat16 [8192, 1024], P('dp', 'seq'), may hold values from -0.0625 to 0.0625
- value_matrix: bfloat16 [8192, 1024], P('dp', 'seq'), may hold values from -0.0625 to 0.0625
- out_grad: bfloat16 [8, 2, 256, 4096], P('dp', None, 'seq'), may hold values from -6 to 6
Outputs:
- attn_out: bfloat16 [8, 2, 256, 4096], P('dp', None, 'seq')
- query_grad: bfloat16 [8, 2, 256, 4096], P('dp', None, 'seq')
- key_weight_grad: float32 [8192, 1024], P('dp', 'seq')
- value_weight_grad: float32 [8192, 1024], P('dp', 'seq')
All inputs are finite; a program needn't handle non-finite values.
Results may differ from a plain program's by a relative error of at most 0.025.
The roundings to bfloat16 on the way count: a program that leaves them out, or rounds other values in their place, can miss the bound.
Values may be sent and summed in bfloat16 or wider, within the bound.
A program may use at most 128 MiB of HBM per device.

v0:
```python
import math

import jax
import jax.numpy as jnp
from jax import lax
from jax.sharding import PartitionSpec as P

QUERY_HEADS_HALF = 32
KEY_VALUE_HEADS = 8
HEAD_WIDTH = 128
STRETCHES = 2


ROPE_BASE = 500000.0


def angle_tables(count, model_head):
    places = jnp.arange(count, dtype=jnp.float32)
    inverse = jnp.exp(
        jnp.arange(model_head // 2, dtype=jnp.float32) * (-2.0 * math.log(ROPE_BASE) / model_head)
    )
    phase_table = places[:, None] * inverse[None, :]
    return (jnp.cos(phase_table), jnp.sin(phase_table))


def rotate(vector, cosine_lookup, sine_lookup):
    half_width = vector.shape[-1] // 2
    first_half = vector[..., :half_width]
    second_half = vector[..., half_width:]
    return jnp.concatenate(
        [
            first_half * cosine_lookup - second_half * sine_lookup,
            second_half * cosine_lookup + first_half * sine_lookup,
        ],
        axis=-1,
    )


def unrotate_gradient(vector, cosine_lookup, sine_lookup):
    half_width = vector.shape[-1] // 2
    first_half = vector[..., :half_width]
    second_half = vector[..., half_width:]
    return jnp.concatenate(
        [
            first_half * cosine_lookup + second_half * sine_lookup,
            second_half * cosine_lookup - first_half * sine_lookup,
        ],
        axis=-1,
    )


def attend(query_block, key_cache, row_offset, score_scale):
    scores = (
        jnp.einsum("tkgd,skd->kgts", query_block, key_cache, preferred_element_type=jnp.float32)
        * score_scale
    )
    row_place = row_offset + jnp.arange(query_block.shape[0])[:, None]
    col_place = jnp.arange(key_cache.shape[0])[None, :]
    scores = jnp.where((col_place <= row_place)[None, None], scores, -jnp.inf)
    row_peak = jnp.max(scores, axis=-1, keepdims=True)
    exp_scores = jnp.exp(scores - row_peak)
    return exp_scores / jnp.sum(exp_scores, axis=-1, keepdims=True)


def local(hidden, queries, key_matrix, value_matrix, out_grad):
    heads_per_group = QUERY_HEADS_HALF // KEY_VALUE_HEADS
    local_tok = hidden.shape[2]
    stretch_len = local_tok * lax.axis_size("seq")
    combined_length = STRETCHES * stretch_len
    score_scale = 1.0 / math.sqrt(HEAD_WIDTH)
    key_full, value_full = (
        lax.all_gather(key_matrix, "dp", axis=0, tiled=True),
        lax.all_gather(value_matrix, "dp", axis=0, tiled=True),
    )
    kv_width = key_full.shape[1]
    local_kv = kv_width // HEAD_WIDTH
    joint_weight = jnp.concatenate([key_full, value_full], axis=1)
    gathered = lax.all_gather(hidden, "seq", axis=2, tiled=True)
    projected = jnp.einsum(
        "bctd,dk->bctk", gathered, joint_weight, preferred_element_type=jnp.float32
    )
    projected = projected.reshape(combined_length, 2 * kv_width)
    cosine_lookup, sine_lookup = angle_tables(combined_length, HEAD_WIDTH)
    cosine_lookup = cosine_lookup[:, None, :]
    sine_lookup = sine_lookup[:, None, :]
    key_projected_raw = projected[:, :kv_width].reshape(combined_length, local_kv, HEAD_WIDTH)
    key_cache = rotate(key_projected_raw, cosine_lookup, sine_lookup).astype(jnp.bfloat16)
    cached_values = (
        projected[:, kv_width:].astype(jnp.bfloat16).reshape(combined_length, local_kv, HEAD_WIDTH)
    )
    query_heads = lax.all_to_all(queries, "seq", split_axis=3, concat_axis=2, tiled=True)[0]
    prob_list = []
    prob_half_list = []
    query_list = []
    output_list = []
    for block_index in range(STRETCHES):
        query_block = query_heads[block_index]
        query_block = query_block.reshape(stretch_len, local_kv, heads_per_group, HEAD_WIDTH)
        key_span = (block_index + 1) * stretch_len
        prob_full = attend(
            query_block, key_cache[:key_span], block_index * stretch_len, score_scale
        )
        prob_half = prob_full.astype(jnp.bfloat16)
        attended = jnp.einsum(
            "kgts,skd->tkgd",
            prob_half,
            cached_values[:key_span],
            preferred_element_type=jnp.float32,
        ).astype(jnp.bfloat16)
        prob_list.append(prob_full)
        prob_half_list.append(prob_half)
        query_list.append(query_block)
        output_list.append(attended)
    stacked_out = jnp.stack([block.reshape(stretch_len, -1) for block in output_list])[None]
    attn_out = lax.all_to_all(stacked_out, "seq", split_axis=2, concat_axis=3, tiled=True)
    grad_heads = lax.all_to_all(out_grad, "seq", split_axis=3, concat_axis=2, tiled=True)[0]
    key_gradient = jnp.zeros((combined_length, local_kv, HEAD_WIDTH), jnp.float32)
    value_gradient = jnp.zeros((combined_length, local_kv, HEAD_WIDTH), jnp.float32)
    query_grad_list = [None] * STRETCHES
    grad_terms = []
    key_weight_grad = None
    value_weight_grad = None
    for block_index in reversed(range(STRETCHES)):
        grad_block = grad_heads[block_index]
        grad_block = grad_block.reshape(stretch_len, local_kv, heads_per_group, HEAD_WIDTH)
        key_span = (block_index + 1) * stretch_len
        grad_prob = jnp.einsum(
            "tkgd,skd->kgts",
            grad_block,
            cached_values[:key_span],
            preferred_element_type=jnp.float32,
        )
        row_dot = jnp.einsum(
            "tkgd,tkgd->kgt",
            grad_block,
            output_list[block_index],
            preferred_element_type=jnp.float32,
        )
        grad_score = (
            prob_list[block_index] * (grad_prob - row_dot[..., None]) * score_scale
        ).astype(jnp.bfloat16)
        query_grad_block = jnp.einsum(
            "kgts,skd->tkgd", grad_score, key_cache[:key_span], preferred_element_type=jnp.float32
        ).astype(jnp.bfloat16)
        key_gradient = key_gradient.at[:key_span].add(
            jnp.einsum(
                "kgts,tkgd->skd",
                grad_score,
                query_list[block_index],
                preferred_element_type=jnp.float32,
            )
        )
        value_gradient = value_gradient.at[:key_span].add(
            jnp.einsum(
                "kgts,tkgd->skd",
                prob_half_list[block_index],
                grad_block,
                preferred_element_type=jnp.float32,
            )
        )
        query_grad_list[block_index] = query_grad_block.reshape(stretch_len, -1)
        row_start = block_index * stretch_len
        key_rows = key_gradient[row_start : row_start + stretch_len]
        value_rows = value_gradient[row_start : row_start + stretch_len]
        weight_row_start = block_index * stretch_len
        cos_rows = cosine_lookup[weight_row_start : weight_row_start + stretch_len]
        sin_rows = sine_lookup[weight_row_start : weight_row_start + stretch_len]
        key_unrotated = (
            unrotate_gradient(key_rows, cos_rows, sin_rows)
            .astype(jnp.bfloat16)
            .reshape(stretch_len, kv_width)
        )
        value_projected = value_rows.astype(jnp.bfloat16).reshape(stretch_len, kv_width)
        joint_grad = jnp.concatenate([key_unrotated, value_projected], axis=1)
        grad_term = jnp.einsum(
            "td,tk->dk", gathered[0, block_index], joint_grad, preferred_element_type=jnp.float32
        )
        grad_terms.append(grad_term)
    grad_total = grad_terms[0]
    for grad_term in grad_terms[1:]:
        grad_total = grad_total + grad_term
    key_weight_grad, value_weight_grad = (
        lax.psum_scatter(grad_total[:, :kv_width], "dp", scatter_dimension=0, tiled=True),
        lax.psum_scatter(grad_total[:, kv_width:], "dp", scatter_dimension=0, tiled=True),
    )
    query_grad = lax.all_to_all(
        jnp.stack(query_grad_list)[None], "seq", split_axis=2, concat_axis=3, tiled=True
    )
    return (attn_out, query_grad, key_weight_grad, value_weight_grad)


def solution(mesh):
    return jax.shard_map(
        local,
        mesh=mesh,
        in_specs=(
            P("dp", None, "seq", None),
            P("dp", None, "seq", None),
            P("dp", "seq"),
            P("dp", "seq"),
            P("dp", None, "seq", None),
        ),
        out_specs=(
            P("dp", None, "seq", None),
            P("dp", None, "seq", None),
            P("dp", "seq"),
            P("dp", "seq"),
        ),
        check_vma=False,
    )
```

profile of v0, /device:TPU:8, one launch (start us, length us, event | category | flops | bytes accessed | tf_op | source)
XLA Modules:
  0.0 460.7 jit_solution(7025641998863762575)
XLA Ops:
  9.4 5.0 %copy.115 = bf16[1,2,64,4096]{2,1,0,3:T(2,128)(2,1)S(1)} copy(bf16[1,2,64,4096]{3,2,1,0:T(8,128)(2,1)} %param.18) | data formatting | bytes 2097152 | tf_op args[1]
  14.4 2.7 reshape.283
  17.1 3.7 all-to-all-start
  20.8 5.0 %copy.126 = bf16[1,2,64,4096]{2,1,0,3:T(2,128)(2,1)S(1)} copy(bf16[1,2,64,4096]{3,2,1,0:T(8,128)(2,1)} %param.21) | data formatting | bytes 2097152 | tf_op args[4]
  25.9 2.7 reshape.285
  28.5 1.0 fusion.36
  29.5 5.0 %all-to-all-done = bf16[4,2,65536]{2,1,0:T(2,128)(2,1)S(1)} async-done(((bf16[4,2,65536]{2,1,0:T(2,128)(2,1)}), bf16[4,2,65536]{2,1,0:T(2,128)(2,1)S(1)}, u32[]{:S(2)}, u32[]{:S(2)}) %all-to-all-start) | async-done | bytes 1048608 | tf_op jit(solution)/shard_map/all_to_all | solution.py:91
  34.5 3.5 all-to-all-start.2
  38.1 0.7 copy.148
  38.8 0.7 copy.142
  39.6 0.7 copy.143
  40.3 0.7 copy.149
  41.6 0.7 iota_compare_fusion
  42.4 3.1 reshape.284
  45.5 3.5 copy.116
  49.0 1.3 fusion.54
  50.6 1.2 copy.147
  52.2 1.1 copy.141
  53.3 1.4 reshape.286
  54.8 1.6 copy.127
  56.9 1.1 copy.151
  58.3 1.1 copy.145
  59.5 44.2 %all-gather.6.cloned.1.call-done = bf16[8192,256]{1,0:T(8,128)(2,1)} async-done(((bf16[1024,256]{1,0:T(8,128)(2,1)}), bf16[8192,256]{1,0:T(8,128)(2,1)}) %all-gather.6.cloned.1.call-update) | async-done | bytes 4194320 | tf_op jit(solution)/shard_map/all_gather | solution.py:73
  103.7 89.4 %all-gather.8.cloned.1.call-done = bf16[1,2,256,8192]{3,2,1,0:T(8,128)(2,1)} async-done(((bf16[1,2,64,8192]{3,2,1,0:T(8,128)(2,1)}), bf16[1,2,256,8192]{3,2,1,0:T(8,128)(2,1)}) %all-gather.8.cloned.1.call-update) | async-done | bytes 8388624 | tf_op jit(solution)/shard_map/all_gather | solution.py:78
  193.1 10.3 %fusion.2 = f32[512,2,256]{0,2,1:T(8,128)S(1)} fusion(bf16[8192,256]{1,0:T(8,128)(2,1)} %all-gather.6.cloned.1.call-done, bf16[8192,256]{1,0:T(8,128)(2,1)} %all-gather.4.cloned.1.call-done, bf16[1,2,256,8192]{3,2,1,0:T(8,128)(2,1)} %all-gather.8.cloned.1.call-done), kind=kOutput, calls=%fused_computation.4 | convolution fusion | flops 4311744512 | bytes 17825792 | tf_op jit(solution)/shard_map/bctd,dk->bctk/dot_general | solution.py:79
  203.6 0.8 copy.119
  204.4 0.8 copy.111
  205.2 0.8 slice.216
  206.0 1.2 copy.196
  207.9 3.5 fusion.59
  211.4 1.8 fusion.28
  213.2 1.5 bitcast_convert_fusion.1
  214.7 1.8 copy.166
  216.5 1.6 multiply_reduce_fusion.1
  218.0 1.7 copy.167
  219.7 4.6 fusion.58
  224.3 2.6 fusion.18
  227.0 0.8 convolution_bitcast_fusion
  229.5 1.8 bitcast_convert_fusion
  231.3 1.7 copy.176
  233.0 0.9 multiply_reduce_fusion
  234.0 3.4 fusion.9
  237.5 0.8 fusion.62
  239.0 10.4 %fusion.6 = f32[512,8192]{1,0:T(8,128)} fusion(bf16[1,2,256,8192]{3,2,1,0:T(8,128)(2,1)} %all-gather.8.cloned.1.call-done, bf16[256,256]{0,1:T(8,128)(2,1)S(1)} %bitcast.224, bf16[256,256]{0,1:T(8,128)(2,1)S(1)} %bitcast.229), kind=kOutput, calls=%fused_computation.10 | convolution fusion | flops 2148007936 | bytes 21233664 | tf_op jit(solution)/shard_map/td,tk->dk/dot_general | solution.py:175
  249.4 13.9 %add_bitcast_fusion = f32[8192,512]{0,1:T(8,128)} fusion(f32[512,8192]{1,0:T(8,128)} %fusion.6, bf16[1,2,256,8192]{3,2,1,0:T(8,128)(2,1)S(1)} %bitcast.207, bf16[256,256]{0,1:T(8,128)(2,1)S(1)} %bitcast.226, bf16[256,256]{0,1:T(8,128)(2,1)S(1)} %bitcast.225), kind=kOutput, calls=%fused_computation.2 | convolution fusion | flops 2152202240 | bytes 38010880 | tf_op jit(solution)/shard_map/td,tk->dk/dot_general | solution.py:175
  263.3 11.2 %fusion.52 = (f32[8192,256]{0,1:T(8,128)}, f32[8192,256]{0,1:T(8,128)}) fusion(f32[8192,512]{0,1:T(8,128)} %add_bitcast_fusion), kind=kLoop, calls=%fused_computation.89 | loop fusion | bytes 33554432 | tf_op jit(solution)/shard_map/slice | solution.py:184
  275.1 2.5 copy.122
  277.6 3.6 copy.123
  281.2 4.3 maximum_bitcast_fusion.2
  285.5 4.5 all-to-all-start.1
  290.0 2.5 convolution_convert_fusion
  292.5 2.5 copy.136
  295.0 2.3 convolution_convert_fusion.2
  297.3 2.5 copy.137
  299.8 3.2 maximum_bitcast_fusion.3
  303.6 3.5 all-to-all-start.3
  307.1 1.5 copy.124
  308.6 1.1 copy.199
  309.7 10.7 %all-to-all-done.3 = bf16[1,2,256,1024]{3,1,0,2:T(2,128)(2,1)S(1)} async-done(((bf16[1,2,256,1024]{3,1,0,2:T(2,128)(2,1)}), bf16[1,2,256,1024]{3,1,0,2:T(2,128)(2,1)S(1)}, u32[]{:S(2)}, u32[]{:S(2)}) %all-to-all-start.3) | async-done | bytes 1048608 | tf_op jit(solution)/shard_map/all_to_all | solution.py:186
  320.6 1.1 copy.200
  321.7 39.7 %reduce-scatter.5.cloned.1.call-done = f32[1024,256]{0,1:T(8,128)} async-done(((f32[8192,256]{0,1:T(8,128)}), f32[1024,256]{0,1:T(8,128)}) %reduce-scatter.5.cloned.1.call-update) | async-done | bytes 1048592 | tf_op jit(solution)/shard_map/reduce_scatter | solution.py:184
  361.4 2.5 copy.153
  363.9 87.7 %reduce-scatter.3.cloned.1.call-done = f32[1024,256]{0,1:T(8,128)} async-done(((f32[8192,256]{0,1:T(8,128)}), f32[1024,256]{0,1:T(8,128)}) %reduce-scatter.3.cloned.1.call-update) | async-done | bytes 1048592 | tf_op jit(solution)/shard_map/reduce_scatter | solution.py:183
  451.6 2.5 copy.152
  (90 shorter events, 9.0 us)
Async XLA Ops:
  7.2 52.3 %all-gather.4.cloned.1.call-start = ((), (), s32[]{:S(2)}) async-start(), calls=%async_computation.6 | async-start | bytes 4718592 | tf_op jit(solution)/shard_map/all_gather | solution.py:72
  7.9 95.8 %all-gather.6.cloned.1.call-start = ((), (), s32[]{:S(2)}) async-start(), calls=%async_computation.7 | async-start | bytes 4718592 | tf_op jit(solution)/shard_map/all_gather | solution.py:73
  8.6 184.5 %all-gather.8.cloned.1.call-start = ((), (), s32[]{:S(2)}) async-start(), calls=%async_computation.8 | async-start | bytes 10485760 | tf_op jit(solution)/shard_map/all_gather | solution.py:78
  17.1 17.4 %all-to-all-start = ((bf16[4,2,65536]{2,1,0:T(2,128)(2,1)}), bf16[4,2,65536]{2,1,0:T(2,128)(2,1)S(1)}, u32[]{:S(2)}, u32[]{:S(2)}) async-start(bf16[4,2,65536]{2,1,0:T(2,128)(2,1)} %reshape.283), calls=%async_computation | async-start | bytes 2097152 | tf_op jit(solution)/shard_map/all_to_all | solution.py:91
  29.5 12.1 %copy-start.2 = (f32[512,64]{1,0:T(8,128)}, f32[512,64]{1,0:T(8,128)S(1)}, u32[]{:S(2)}) copy-start(f32[512,64]{1,0:T(8,128)S(1)} %get-tuple-element.103) | copy-start | bytes 393220
  34.5 7.1 %copy-start = (bf16[4,2,65536]{2,1,0:T(2,128)(2,1)}, bf16[4,2,65536]{2,1,0:T(2,128)(2,1)S(1)}, u32[]{:S(2)}) copy-start(bf16[4,2,65536]{2,1,0:T(2,128)(2,1)S(1)} %all-to-all-done) | copy-start | bytes 3145732
  34.5 18.8 %all-to-all-start.2 = ((bf16[4,2,65536]{2,1,0:T(2,128)(2,1)}), bf16[4,2,65536]{2,1,0:T(2,128)(2,1)S(1)}, u32[]{:S(2)}, u32[]{:S(2)}) async-start(bf16[4,2,65536]{2,1,0:T(2,128)(2,1)} %reshape.285), calls=%async_computation.2 | async-start | bytes 2097152 | tf_op jit(solution)/shard_map/all_to_all | solution.py:116
  38.0 323.4 %reduce-scatter.5.cloned.1.call-start = ((), (), s32[]{:S(2)}) async-start(), calls=%async_computation.10 | async-start | bytes 9437184 | tf_op jit(solution)/shard_map/reduce_scatter | solution.py:184
  203.4 4.3 copy-start.3
  207.9 6.8 %copy-start.4 = (bf16[512,2,64]{2,0,1:T(8,128)(2,1)}, bf16[512,2,64]{2,0,1:T(8,128)(2,1)S(1)}, u32[]{:S(2)}) copy-start(bf16[512,2,64]{2,0,1:T(8,128)(2,1)S(1)} %get-tuple-element.86) | copy-start | bytes 393220
  207.9 6.8 %copy-start.6 = (bf16[512,2,64]{2,0,1:T(8,128)(2,1)}, bf16[512,2,64]{2,0,1:T(8,128)(2,1)S(1)}, u32[]{:S(2)}) copy-start(bf16[512,2,64]{2,0,1:T(8,128)(2,1)S(1)} %get-tuple-element.87) | copy-start | bytes 393220
  207.9 5.3 %copy-start.14 = (bf16[256,256]{0,1:T(8,128)(2,1)S(1)}, bf16[256,256]{0,1:T(8,128)(2,1)}, u32[]{:S(2)}) copy-start(bf16[256,256]{0,1:T(8,128)(2,1)} %copy.111) | copy-start | bytes 393220
  213.1 6.5 %copy-start.20 = (pred[256,512]{0,1:T(8,128)(4,1)S(1)}, pred[256,512]{0,1:T(8,128)(4,1)}, u32[]{:S(2)}) copy-start(pred[256,512]{0,1:T(8,128)(4,1)} %iota_compare_fusion) | copy-start | bytes 393220
  214.7 5.0 %copy-start.5 = (bf16[512,2,64]{2,0,1:T(8,128)(2,1)S(1)}, bf16[512,2,64]{2,0,1:T(8,128)(2,1)}, u32[]{:S(2)}) copy-start(bf16[512,2,64]{2,0,1:T(8,128)(2,1)} %copy-done.4) | copy-start | bytes 393220
  224.3 2.6 copy-start.10
  224.3 3.5 copy-start.11
  226.9 1.6 copy-start.7
  226.9 1.6 copy-start.15
  227.0 1.6 copy-start.21
  227.8 3.5 copy-start.13
  228.5 1.0 copy-start.12
  229.1 9.2 %copy-start.1 = (bf16[2,4,256,256]{2,3,1,0:T(8,128)(2,1)}, bf16[2,4,256,256]{2,3,1,0:T(8,128)(2,1)S(1)}, u32[]{:S(2)}) copy-start(bf16[2,4,256,256]{2,3,1,0:T(8,128)(2,1)S(1)} %fusion.13) | copy-start | bytes 3145732
  234.0 3.4 copy-start.9
  234.0 4.3 copy-start.8
  237.4 1.4 copy-start.18
  237.4 1.4 copy-start.19
  237.4 1.4 copy-start.16
  237.5 1.4 copy-start.17
  237.5 1.5 slice-start.2
  238.8 10.6 %slice-start = ((s8[8388608]{0:T(1024)(128)(4,1)}), s8[4194304]{0:T(1024)(128)(4,1)S(1)}, s32[]{:S(2)}) async-start(s8[8388608]{0:T(1024)(128)(4,1)} %bitcast.206), calls=%async_computation.11 | async-start | bytes 8388608
  239.0 10.5 %slice-start.1 = ((s8[8388608]{0:T(1024)(128)(4,1)}), s8[4194304]{0:T(1024)(128)(4,1)S(1)}, s32[]{:S(2)}) async-start(s8[8388608]{0:T(1024)(128)(4,1)} %bitcast.206), calls=%async_computation.12 | async-start | bytes 8388608
  274.5 177.1 %reduce-scatter.3.cloned.1.call-start = ((), (), s32[]{:S(2)}) async-start(), calls=%async_computation.9 | async-start | bytes 9437184 | tf_op jit(solution)/shard_map/reduce_scatter | solution.py:183
  285.5 18.1 %all-to-all-start.1 = ((bf16[1,2,256,1024]{3,1,0,2:T(2,128)(2,1)}), bf16[1,2,256,1024]{3,1,0,2:T(2,128)(2,1)}, u32[]{:S(2)}, u32[]{:S(2)}) async-start(bf16[1,2,256,1024]{3,1,0,2:T(2,128)(2,1)} %maximum_bitcast_fusion.2), calls=%async_computation.1 | async-start | bytes 2097152 | tf_op jit(solution)/shard_map/all_to_all | solution.py:115
  303.6 16.8 %all-to-all-start.3 = ((bf16[1,2,256,1024]{3,1,0,2:T(2,128)(2,1)}), bf16[1,2,256,1024]{3,1,0,2:T(2,128)(2,1)S(1)}, u32[]{:S(2)}, u32[]{:S(2)}) async-start(bf16[1,2,256,1024]{3,1,0,2:T(2,128)(2,1)} %maximum_bitcast_fusion.3), calls=%async_computation.3 | async-start | bytes 2097152 | tf_op jit(solution)/shard_map/all_to_all | solution.py:186
Sparse Core Ops, SparseCore 0:
  9.6 46.7 all-gather.3
  58.0 45.6 all-gather.5
  105.5 87.5 all-gather.7
  274.6 86.7 reduce-scatter.4
  363.6 88.0 reduce-scatter.2
where the time goes:
time: 466 us; the launch traced here: 461 us
  waiting for transfers between devices  280 us (60%)
  local copies, waits for them, and re-layouts  76.6 us (16%)
  matrix products  57.3 us (12%)
  other arithmetic  17 us (4%)
  starting transfers between devices  15.5 us (3%)
  between operations  14.4 us (3%)
    all_gather x1, waiting for transfers between devices, local(): gathered = lax.all_gather(hidden, 'seq', axis=2, tiled=True)  89.4 us
    reduce_scatter x1, waiting for transfers between devices, local(): lax.psum_scatter(grad_total[:, :kv_width], 'dp', scatter_dimension=0, til...  87.7 us
    all_gather x1, waiting for transfers between devices, local(): lax.all_gather(value_matrix, 'dp', axis=0, tiled=True)  44.2 us
    reduce_scatter x1, waiting for transfers between devices, local(): lax.psum_scatter(grad_total[:, kv_width:], 'dp', scatter_dimension=0, til...  39.7 us
    unnamed x61, local copies, waits for them, and re-layouts  30.8 us
    dot_general x2, matrix products, local(): jnp.einsum('td,tk->dk', gathered[0, block_index], joint_grad, preferred_e...  24.3 us
    slice x1, local copies, waits for them, and re-layouts, local(): grad_total[:, kv_width:]  11.2 us
    all_to_all x1, waiting for transfers between devices, local(): lax.all_to_all(jnp.stack(query_grad_list)[None], 'seq', split_axis=2, con...  10.7 us
  transfers between devices with their start and end apart: 9, of which 7 were waited for; matrix products, arithmetic and copies ran while one was open for 15% of the time, Pallas kernels for 0%

commit v1 on v0

v1 whole, which is shorter than its diff:
```python
import functools
import math

import jax
import jax.numpy as jnp
import numpy as np
from jax import lax
from jax.experimental import pallas as pl
from jax.experimental.pallas import tpu as pltpu
from jax.sharding import PartitionSpec as P

HEAD_WIDTH = 128
ROPE_BASE = 500000.0
CORES = 2
MESH = pl.DeviceIdType.MESH
ANY = pl.BlockSpec(memory_space=pl.ANY)
VMEM = pl.BlockSpec(memory_space=pltpu.VMEM)
VMEM_LIMIT = 60 << 20


def grid_of(count):
    rows = 2 if count % 2 == 0 else 1
    return rows, count // rows


def place(n_seq, n_dp):
    dp, seq = lax.axis_index("dp"), lax.axis_index("seq")
    chips = n_dp // CORES
    chip, core = lax.div(dp, CORES), lax.rem(dp, CORES)
    rows, cols = grid_of(n_seq)
    row, col = lax.div(seq, cols), lax.rem(seq, cols)
    row_peers = [row * cols + lax.rem(col + d, cols) for d in range(1, cols)]
    col_peers = [lax.rem(row + d, rows) * cols + col for d in range(1, rows)]
    far_peers = [
        lax.rem(row + e, rows) * cols + lax.rem(col + d, cols)
        for e in range(1, rows)
        for d in range(1, cols)
    ]
    return dp, seq, chips, chip, core, row_peers, col_peers, far_peers


def greet(dp, seq, chips, chip, core, peers):
    barrier = pltpu.get_barrier_semaphore()
    ids = [(dp, p) for p in peers]
    ids.append((chip * CORES + 1 - core, seq))
    if chips > 1:
        for d in (1, chips - 1):
            ids.append((lax.rem(chip + d, chips) * CORES + core, seq))
    for device in ids:
        pl.semaphore_signal(barrier, inc=1, device_id=device, device_id_type=MESH)
    pl.semaphore_wait(barrier, len(ids))


def gather_kernel(
    n_seq, n_dp, hidden, queries, key_matrix, value_matrix, out_grad,
    hid_all, qry_all, grd_all, key_all, val_all,
    hid_own, qry_own, grd_own, key_own, val_own,
    load_sem, store_sem, hid_send, hid_recv, qry_send, qry_recv, grd_send, grd_recv,
    up_send, down_send, mate_send, w_recv,
):
    dp, seq, chips, chip, core, row_peers, col_peers, far_peers = place(n_seq, n_dp)
    peers = row_peers + col_peers + far_peers
    width = qry_own.shape[2]
    mine = pl.ds(pl.multiple_of(seq * width, width), width)
    local_pairs = (
        (hidden, hid_own, hid_all.at[:, seq]),
        (queries.at[:, :, mine], qry_own, qry_all.at[:, seq]),
        (out_grad.at[:, :, mine], grd_own, grd_all.at[:, seq]),
        (key_matrix, key_own, key_all.at[dp]),
        (value_matrix, val_own, val_all.at[dp]),
    )
    for i, (src, tmp, _) in enumerate(local_pairs):
        pltpu.make_async_copy(src, tmp, load_sem.at[i]).start()
    greet(dp, seq, chips, chip, core, peers)
    sends = []
    slots = iter(range(hid_send.shape[0]))

    def send_hidden(source, half, target, src):
        copy = pltpu.make_async_remote_copy(
            src_ref=src, dst_ref=hid_all.at[half, source],
            send_sem=hid_send.at[next(slots)], recv_sem=hid_recv.at[source, half],
            device_id=(dp, target), device_id_type=MESH,
        )
        copy.start()
        sends.append(copy)

    def wait_hidden(source, half):
        pltpu.make_async_remote_copy(
            src_ref=hid_all.at[half, source], dst_ref=hid_all.at[half, source],
            send_sem=hid_send.at[0], recv_sem=hid_recv.at[source, half],
            device_id=(dp, source), device_id_type=MESH,
        ).wait_recv()

    tables = (key_all, val_all)
    owns = (key_matrix, value_matrix)

    def weight_copy(kind, piece, target_dp, send_sem, own=False):
        return pltpu.make_async_remote_copy(
            src_ref=owns[kind] if own else tables[kind].at[piece],
            dst_ref=tables[kind].at[piece],
            send_sem=send_sem, recv_sem=w_recv.at[piece, kind],
            device_id=(target_dp, seq), device_id_type=MESH,
        )

    above, below = dp + CORES, dp - CORES
    mate = chip * CORES + 1 - core
    has_above, has_below = chip < chips - 1, chip > 0

    def go(cond, copy_of, wait=False):
        @pl.when(cond)
        def _():
            copy = copy_of()
            copy.wait_send() if wait else copy.start()

    for p in row_peers:
        send_hidden(seq, 0, p, hidden.at[0])
    for p in col_peers:
        send_hidden(seq, 1, p, hidden.at[1])
    for kind in range(2):
        go(has_above, lambda: weight_copy(kind, dp, above, up_send.at[0, kind], True))
        go(has_below, lambda: weight_copy(kind, dp, below, down_send.at[0, kind], True))
    for p in row_peers:
        send_hidden(seq, 1, p, hidden.at[1])
    for p in col_peers:
        send_hidden(seq, 0, p, hidden.at[0])
    for kind in range(2):
        weight_copy(kind, dp, mate, mate_send.at[dp, kind], True).start()
    for i, (src, tmp, dst) in enumerate(local_pairs):
        pltpu.make_async_copy(src, tmp, load_sem.at[i]).wait()
        pltpu.make_async_copy(tmp, dst, store_sem.at[i]).start()

    def relay_weight(step, kind):
        low, high = dp - CORES * step, dp + CORES * step

        @pl.when(chip >= step)
        def _():
            weight_copy(kind, low, below, up_send.at[step, kind]).wait_recv()
            go(has_above, lambda: weight_copy(kind, low, above, up_send.at[step, kind]))
            weight_copy(kind, low, mate, mate_send.at[low, kind]).start()

        @pl.when(chip + step < chips)
        def _():
            weight_copy(kind, high, above, down_send.at[step, kind]).wait_recv()
            go(has_below, lambda: weight_copy(kind, high, below, down_send.at[step, kind]))
            weight_copy(kind, high, mate, mate_send.at[high, kind]).start()

    def relay_hidden():
        for p in row_peers:
            wait_hidden(p, 0)
            for q in col_peers:
                send_hidden(p, 0, q, hid_all.at[0, p])
        for p in col_peers:
            wait_hidden(p, 1)
            for q in row_peers:
                send_hidden(p, 1, q, hid_all.at[1, p])

    def exchange(src, dst, send_sem, recv_sem):
        for i, p in enumerate(peers):
            cols = pl.ds(pl.multiple_of(p * width, width), width)
            copy = pltpu.make_async_remote_copy(
                src_ref=src.at[:, :, cols], dst_ref=dst.at[:, seq],
                send_sem=send_sem.at[i], recv_sem=recv_sem.at[seq],
                device_id=(dp, p), device_id_type=MESH,
            )
            copy.start()
            sends.append(copy)

    def wait_exchange(dst, send_sem, recv_sem):
        for p in peers:
            pltpu.make_async_remote_copy(
                src_ref=dst.at[:, p], dst_ref=dst.at[:, p],
                send_sem=send_sem.at[0], recv_sem=recv_sem.at[p],
                device_id=(dp, p), device_id_type=MESH,
            ).wait_recv()

    if chips > 1:
        relay_weight(1, 0)
    relay_hidden()
    exchange(queries, qry_all, qry_send, qry_recv)
    exchange(out_grad, grd_all, grd_send, grd_recv)
    if chips > 1:
        relay_weight(1, 1)
    for step in range(2, chips):
        for kind in range(2):
            relay_weight(step, kind)
    for p in row_peers:
        wait_hidden(p, 1)
    for p in col_peers:
        wait_hidden(p, 0)
    for p in far_peers:
        wait_hidden(p, 0)
        wait_hidden(p, 1)
    wait_exchange(qry_all, qry_send, qry_recv)
    wait_exchange(grd_all, grd_send, grd_recv)
    for other in range(chips):
        for kind in range(2):
            piece = other * CORES + 1 - core
            weight_copy(kind, piece, mate, mate_send.at[piece, kind]).wait_recv()
    for copy in sends:
        copy.wait_send()
    for kind in range(2):
        for step in range(max(chips - 1, 1)):
            low, high = dp - CORES * step, dp + CORES * step
            go(jnp.logical_and(has_above, chip >= step),
               lambda: weight_copy(kind, low, above, up_send.at[step, kind]), True)
            go(jnp.logical_and(has_below, chip + step < chips),
               lambda: weight_copy(kind, high, below, down_send.at[step, kind]), True)
        for other in range(chips):
            piece = other * CORES + core
            weight_copy(kind, piece, mate, mate_send.at[piece, kind]).wait_send()
    for i, (_, tmp, dst) in enumerate(local_pairs):
        pltpu.make_async_copy(tmp, dst, store_sem.at[i]).wait()


def gather_all(n_seq, n_dp, hidden, queries, key_matrix, value_matrix, out_grad):
    _, stretches, tokens, embed = hidden.shape
    width = queries.shape[3] // n_seq
    chips = n_dp // CORES
    rows, cols = grid_of(n_seq)
    hid_sends = 2 * (rows - 1 + cols - 1) + 2 * (rows - 1) * (cols - 1)
    bf16 = jnp.bfloat16
    dma = pltpu.SemaphoreType.DMA
    heads = (stretches, n_seq, tokens, width)
    own = (stretches, tokens, width)
    weight = key_matrix.shape
    return pl.pallas_call(
        functools.partial(gather_kernel, n_seq, n_dp),
        out_shape=[
            jax.ShapeDtypeStruct((stretches, n_seq, tokens, embed), bf16),
            jax.ShapeDtypeStruct(heads, bf16),
            jax.ShapeDtypeStruct(heads, bf16),
            jax.ShapeDtypeStruct((n_dp,) + weight, bf16),
            jax.ShapeDtypeStruct((n_dp,) + weight, bf16),
        ],
        in_specs=[ANY] * 5,
        out_specs=[ANY] * 5,
        scratch_shapes=[
            pltpu.VMEM((stretches, tokens, embed), bf16),
            pltpu.VMEM(own, bf16),
            pltpu.VMEM(own, bf16),
            pltpu.VMEM(weight, bf16),
            pltpu.VMEM(weight, bf16),
            dma((5,)), dma((5,)),
            dma((hid_sends,)), dma((n_seq, 2)),
            dma((n_seq,)), dma((n_seq,)), dma((n_seq,)), dma((n_seq,)),
            dma((chips, 2)), dma((chips, 2)), dma((n_dp, 2)), dma((n_dp, 2)),
        ],
        compiler_params=pltpu.CompilerParams(
            collective_id=0, has_side_effects=True, vmem_limit_bytes=VMEM_LIMIT
        ),
        name="gather_all",
    )(hidden[0], queries[0], key_matrix, value_matrix, out_grad[0])


def attention_kernel(
    group, key_raw, val_raw, cos, sin, cos_t, sin_t, qry, grd,
    out, qry_grad, pre_t, keys, vals, key_acc, val_acc,
):
    member = pl.program_id(1)
    total = qry.shape[0]
    half = HEAD_WIDTH // 2
    block = total // 2
    scale = 1.0 / math.sqrt(HEAD_WIDTH)
    f32, bf16 = jnp.float32, jnp.bfloat16

    @pl.when(member == 0)
    def _():
        raw = key_raw[...]
        swapped = jnp.concatenate([raw[:, half:], raw[:, :half]], axis=1)
        keys[...] = (raw * cos[...] + swapped * sin[...]).astype(bf16)
        vals[...] = val_raw[...].astype(bf16)
        key_acc[...] = jnp.zeros_like(key_acc)
        val_acc[...] = jnp.zeros_like(val_acc)

    nt = (((1,), (1,)), ((), ()))
    tn = (((0,), (0,)), ((), ()))
    for b in range(2):
        rows = pl.ds(b * block, block)
        span = (b + 1) * block
        q, g = qry[rows, :], grd[rows, :]
        k, v = keys[:span, :], vals[:span, :]
        s = lax.dot_general(q, k, nt, preferred_element_type=f32) * scale
        at = b * block + lax.broadcasted_iota(jnp.int32, s.shape, 0)
        col = lax.broadcasted_iota(jnp.int32, s.shape, 1)
        s = jnp.where(col <= at, s, -jnp.inf)
        e = jnp.exp(s - jnp.max(s, axis=1, keepdims=True))
        p = e * (1.0 / jnp.sum(e, axis=1, keepdims=True))
        p_half = p.astype(bf16)
        o = jnp.dot(p_half, v, preferred_element_type=f32).astype(bf16)
        out[rows, :] = o
        dot = jnp.sum(g.astype(f32) * o.astype(f32), axis=1, keepdims=True)
        gp = lax.dot_general(g, v, nt, preferred_element_type=f32)
        ds = (p * (gp - dot) * scale).astype(bf16)
        qry_grad[rows, :] = jnp.dot(ds, k, preferred_element_type=f32).astype(bf16)
        key_acc[:, :span] += lax.dot_general(q, ds, tn, preferred_element_type=f32)
        val_acc[:, :span] += lax.dot_general(g, p_half, tn, preferred_element_type=f32)

    @pl.when(member == group - 1)
    def _():
        acc = key_acc[...]
        swapped = jnp.concatenate([acc[half:, :], acc[:half, :]], axis=0)
        pre_t[0] = (acc * cos_t[...] - swapped * sin_t[...]).astype(bf16)
        pre_t[1] = val_acc[...].astype(bf16)


def attention(key_raw, val_raw, qry, grd):
    total, width = qry.shape
    kv_width = key_raw.shape[1]
    kv_heads = kv_width // HEAD_WIDTH
    group = width // kv_width
    bf16, f32 = jnp.bfloat16, jnp.float32
    half = HEAD_WIDTH // 2
    inverse = np.exp(
        np.arange(half, dtype=np.float32) * np.float32(-2.0 * math.log(ROPE_BASE) / HEAD_WIDTH)
    ).astype(np.float32)
    phase = np.arange(total, dtype=np.float32)[:, None] * inverse[None, :]
    cos_half, sin_half = np.cos(phase), np.sin(phase)
    cos = np.concatenate([cos_half, cos_half], axis=1).astype(np.float32)
    sin = np.concatenate([-sin_half, sin_half], axis=1).astype(np.float32)
    head = lambda k, m: (0, k * group + m)
    by_kv = lambda k, m: (0, k)
    whole = lambda k, m: (0, 0)
    out, qry_grad, pre_t = pl.pallas_call(
        functools.partial(attention_kernel, group),
        grid=(kv_heads, group),
        in_specs=[
            pl.BlockSpec((total, HEAD_WIDTH), by_kv),
            pl.BlockSpec((total, HEAD_WIDTH), by_kv),
            pl.BlockSpec((total, HEAD_WIDTH), whole),
            pl.BlockSpec((total, HEAD_WIDTH), whole),
            pl.BlockSpec((HEAD_WIDTH, total), whole),
            pl.BlockSpec((HEAD_WIDTH, total), whole),
            pl.BlockSpec((total, HEAD_WIDTH), head),
            pl.BlockSpec((total, HEAD_WIDTH), head),
        ],
        out_specs=[
            pl.BlockSpec((total, HEAD_WIDTH), head),
            pl.BlockSpec((total, HEAD_WIDTH), head),
            pl.BlockSpec((2, HEAD_WIDTH, total), lambda k, m: (0, k, 0)),
        ],
        out_shape=[
            jax.ShapeDtypeStruct((total, width), bf16),
            jax.ShapeDtypeStruct((total, width), bf16),
            jax.ShapeDtypeStruct((2, kv_width, total), bf16),
        ],
        scratch_shapes=[
            pltpu.VMEM((total, HEAD_WIDTH), bf16),
            pltpu.VMEM((total, HEAD_WIDTH), bf16),
            pltpu.VMEM((HEAD_WIDTH, total), f32),
            pltpu.VMEM((HEAD_WIDTH, total), f32),
        ],
        compiler_params=pltpu.CompilerParams(
            dimension_semantics=("arbitrary", "arbitrary"), vmem_limit_bytes=VMEM_LIMIT
        ),
        name="attention",
    )(key_raw, val_raw, cos, sin, cos.T.copy(), sin.T.copy(), qry, grd)
    return out, qry_grad, pre_t.reshape(2 * kv_width, total)


def reduce_kernel(
    n_seq, n_dp, tile, hid, pre_t, attn, qgrad,
    attn_out, qgrad_out, weight_grad,
    attn_own, qgrad_own, acc, mate_out, mate_in, chain_out, down_in, up_in,
    load_sem, store_sem, a_send, a_recv, q_send, q_recv,
    mate_send, mate_recv, chain_send, down_recv, up_recv,
):
    dp, seq, chips, chip, core, row_peers, col_peers, far_peers = place(n_seq, n_dp)
    peers = row_peers + col_peers + far_peers
    width = attn_own.shape[2]
    height, depth = acc.shape[1], acc.shape[2]
    mine = pl.ds(pl.multiple_of(seq * width, width), width)
    local_pairs = (
        (attn.at[:, seq], attn_own, attn_out.at[:, :, mine]),
        (qgrad.at[:, seq], qgrad_own, qgrad_out.at[:, :, mine]),
    )
    for i, (src, tmp, _) in enumerate(local_pairs):
        pltpu.make_async_copy(src, tmp, load_sem.at[i]).start()
    greet(dp, seq, chips, chip, core, peers)
    exchanges = ((attn, attn_out, a_send, a_recv), (qgrad, qgrad_out, q_send, q_recv))
    sends = []
    for src, dst, send_sem, recv_sem in exchanges:
        for i, p in enumerate(peers):
            copy = pltpu.make_async_remote_copy(
                src_ref=src.at[:, p], dst_ref=dst.at[:, :, mine],
                send_sem=send_sem.at[i], recv_sem=recv_sem.at[seq],
                device_id=(dp, p), device_id_type=MESH,
            )
            copy.start()
            sends.append(copy)
    mate = chip * CORES + 1 - core

    def mate_copy(t):
        return pltpu.make_async_remote_copy(
            src_ref=mate_out.at[t], dst_ref=mate_in.at[t],
            send_sem=mate_send.at[t], recv_sem=mate_recv.at[t],
            device_id=(mate, seq), device_id_type=MESH,
        )

    def chain_copy(t, down):
        return pltpu.make_async_remote_copy(
            src_ref=chain_out.at[t], dst_ref=(down_in if down else up_in).at[t],
            send_sem=chain_send.at[t], recv_sem=(down_recv if down else up_recv).at[t],
            device_id=(dp - CORES if down else dp + CORES, seq), device_id_type=MESH,
        )

    def product(block, store):
        @pl.loop(0, depth // tile)
        def _(i):
            cols = pl.ds(pl.multiple_of(block * depth + i * tile, tile), tile)
            part = jnp.dot(pre_t[...], hid[:, cols], preferred_element_type=jnp.float32)
            store(pl.ds(pl.multiple_of(i * tile, tile), tile), part)

    @pl.loop(0, chips)
    def _(i):
        odd, k = lax.rem(i, 2), lax.div(i, 2)
        t = odd * (chips - 1 - k) + (1 - odd) * k

        def to_mate(cols, part):
            mate_out[t, :, cols] = part.astype(jnp.bfloat16)

        def to_acc(cols, part):
            acc[t, :, cols] = part

        product(t * CORES + 1 - core, to_mate)
        mate_copy(t).start()
        product(t * CORES + core, to_acc)

    strip = 64

    def sweep(fn):
        @pl.loop(0, height // strip)
        def _(i):
            fn(pl.ds(pl.multiple_of(i * strip, strip), strip))

    def take(t, extra):
        def fn(rows):
            acc[t, rows, :] += extra[t, rows, :].astype(jnp.float32)

        sweep(fn)

    def relay(t, down, has_input):
        mate_copy(t).wait_recv()
        take(t, mate_in)

        @pl.when(has_input)
        def _():
            chain_copy(t, down).wait_recv()
            take(t, down_in if down else up_in)

        def fn(rows):
            chain_out[t, rows, :] = acc[t, rows, :].astype(jnp.bfloat16)

        sweep(fn)
        chain_copy(t, down).start()

    has_above, has_below = chip < chips - 1, chip > 0

    @pl.loop(0, chips - 1)
    def _(tau):
        k_down = tau - (chips - 1 - chip)
        k_up = tau - chip

        @pl.when(jnp.logical_and(k_down >= 0, k_down < chip))
        def _():
            relay(k_down, True, has_above)

        @pl.when(jnp.logical_and(k_up >= 0, k_up < chips - 1 - chip))
        def _():
            relay(chips - 1 - k_up, False, has_below)

    mate_copy(chip).wait_recv()
    take(chip, mate_in)

    @pl.when(has_above)
    def _():
        chain_copy(chip, True).wait_recv()
        take(chip, down_in)

    @pl.when(has_below)
    def _():
        chain_copy(chip, False).wait_recv()
        take(chip, up_in)

    def finish(rows):
        weight_grad[rows, :] = acc[chip, rows, :]

    sweep(finish)
    for i, (src, tmp, dst) in enumerate(local_pairs):
        pltpu.make_async_copy(src, tmp, load_sem.at[i]).wait()
        pltpu.make_async_copy(tmp, dst, store_sem.at[i]).start()
    for src, dst, send_sem, recv_sem in exchanges:
        for p in peers:
            cols = pl.ds(pl.multiple_of(p * width, width), width)
            pltpu.make_async_remote_copy(
                src_ref=src.at[:, p], dst_ref=dst.at[:, :, cols],
                send_sem=send_sem.at[0], recv_sem=recv_sem.at[p],
                device_id=(dp, p), device_id_type=MESH,
            ).wait_recv()
    for copy in sends:
        copy.wait_send()

    for t in range(chips):
        mate_copy(t).wait_send()

        @pl.when(chip != t)
        def _():
            chain_copy(t, True).wait_send()

    for i, (_, tmp, dst) in enumerate(local_pairs):
        pltpu.make_async_copy(tmp, dst, store_sem.at[i]).wait()


def reduce_all(n_seq, n_dp, hid, pre_t, attn, qgrad):
    stretches, _, tokens, width = attn.shape
    chips = n_dp // CORES
    height = pre_t.shape[0]
    depth = hid.shape[1] // n_dp
    bf16, f32 = jnp.bfloat16, jnp.float32
    dma = pltpu.SemaphoreType.DMA
    out = (stretches, tokens, n_seq * width)
    own = (stretches, tokens, width)
    blocks = (chips, height, depth)
    return pl.pallas_call(
        functools.partial(reduce_kernel, n_seq, n_dp, math.gcd(depth, 256)),
        out_shape=[
            jax.ShapeDtypeStruct(out, bf16),
            jax.ShapeDtypeStruct(out, bf16),
            jax.ShapeDtypeStruct((height, depth), f32),
        ],
        in_specs=[VMEM, VMEM, ANY, ANY],
        out_specs=[ANY, ANY, VMEM],
        scratch_shapes=[
            pltpu.VMEM(own, bf16),
            pltpu.VMEM(own, bf16),
            pltpu.VMEM(blocks, f32),
            pltpu.VMEM(blocks, bf16),
            pltpu.VMEM(blocks, bf16),
            pltpu.VMEM(blocks, bf16),
            pltpu.VMEM(blocks, bf16),
            pltpu.VMEM(blocks, bf16),
            dma((2,)), dma((2,)),
            dma((n_seq,)), dma((n_seq,)), dma((n_seq,)), dma((n_seq,)),
            dma((chips,)), dma((chips,)), dma((chips,)), dma((chips,)), dma((chips,)),
        ],
        compiler_params=pltpu.CompilerParams(
            collective_id=1, has_side_effects=True, vmem_limit_bytes=VMEM_LIMIT
        ),
        name="reduce_all",
    )(hid, pre_t, attn, qgrad)


def local(n_seq, n_dp, hidden, queries, key_matrix, value_matrix, out_grad):
    hid, qry, grd, key_full, val_full = gather_all(
        n_seq, n_dp, hidden, queries, key_matrix, value_matrix, out_grad
    )
    stretches, _, tokens, width = qry.shape
    total = stretches * n_seq * tokens
    embed = hid.shape[-1]
    hid = hid.reshape(total, embed)
    kv_width = key_matrix.shape[1]
    f32 = jnp.float32
    key_raw = jnp.dot(hid, key_full.reshape(embed, kv_width), preferred_element_type=f32)
    val_raw = jnp.dot(hid, val_full.reshape(embed, kv_width), preferred_element_type=f32)
    attn, qgrad, pre_t = attention(
        key_raw, val_raw, qry.reshape(total, width), grd.reshape(total, width)
    )
    attn_out, query_grad, grad_t = reduce_all(
        n_seq, n_dp, hid, pre_t, attn.reshape(qry.shape), qgrad.reshape(qry.shape)
    )
    return attn_out[None], query_grad[None], grad_t[:kv_width].T, grad_t[kv_width:].T


def solution(mesh):
    n_dp, n_seq = mesh.shape["dp"], mesh.shape["seq"]
    tokens, weights = P("dp", None, "seq", None), P("dp", "seq")
    return jax.shard_map(
        functools.partial(local, n_seq, n_dp),
        mesh=mesh,
        in_specs=(tokens, tokens, weights, weights, tokens),
        out_specs=(tokens, tokens, weights, weights),
        check_vma=False,
    )
```

time: 466 us -> 220 us (0.47); the launches traced: 461 us -> 219 us
  waiting for transfers between devices: 280 us -> 0 us
  Pallas kernels: 0 us -> 200 us
  local copies, waits for them, and re-layouts: 76.6 us -> 8.06 us
  matrix products: 57.3 us -> 11 us
  other arithmetic: 17 us -> 0 us
  starting transfers between devices: 15.5 us -> 0 us
  between operations: 14.4 us -> 0.68 us
    pallas_call x0 -> x3, Pallas kernels: none -> 200 us  [the longest x1 95.6 us: gather_all(): pl.pallas_call(functools.partial(gather_kernel, n_seq, n_dp), out_shape=[...]
    all_gather x3 -> x0, waiting for transfers between devices: 134 us -> none  [the longest x1 89.4 us: local(): gathered = lax.all_gather(hidden, 'seq', axis=2, tiled=True)]
    reduce_scatter x2 -> x0, waiting for transfers between devices: 127 us -> none  [the longest x1 87.7 us: local(): lax.psum_scatter(grad_total[:, :kv_width], 'dp', scatter_dimension=0, til...]
    dot_general x13 -> x2, matrix products: 49.3 us -> 11 us  [the longest x1 7.85 us: local(): jnp.dot(hid, val_full.reshape(embed, kv_width), preferred_element_type=f32)]
    unnamed x61 -> x10, local copies, waits for them, and re-layouts: 30.8 us -> 6.33 us
    slice x16 -> x0, local copies, waits for them, and re-layouts: 17.9 us -> none  [the longest x1 11.2 us: local(): grad_total[:, kv_width:]]
    another operation x12 -> x0, local copies, waits for them, and re-layouts: 17 us -> none  [the longest x2 6.06 us: local(): jnp.stack([block.reshape(stretch_len, -1) for block in output_list])[None]]
    all_to_all x4 -> x0, waiting for transfers between devices: 16.2 us -> none  [the longest x1 10.7 us: local(): lax.all_to_all(jnp.stack(query_grad_list)[None], 'seq', split_axis=2, con...]
  transfers between devices with their start and end apart: 9 -> 0, of which waited for: 7 -> 0; matrix products, arithmetic and copies ran while one was open for 15% -> 0% of each run, Pallas kernels for 0% -> 0%
where the time goes in v1:
time: 220 us; the launch traced here: 219 us
  Pallas kernels  200 us (91%)
  matrix products  11 us (5%)
  local copies, waits for them, and re-layouts  8.06 us (4%)
    pallas_call x1, Pallas kernels, gather_all(): pl.pallas_call(functools.partial(gather_kernel, n_seq, n_dp), out_shape=[...  95.6 us
    pallas_call x1, Pallas kernels, reduce_all(): pl.pallas_call(functools.partial(reduce_kernel, n_seq, n_dp, math.gcd(dep...  88.5 us
    pallas_call x1, Pallas kernels, attention(): pl.pallas_call(functools.partial(attention_kernel, group), grid=(kv_heads...  15.6 us
    dot_general x1, matrix products, local(): jnp.dot(hid, val_full.reshape(embed, kv_width), preferred_element_type=f32)  7.85 us
    unnamed x10, local copies, waits for them, and re-layouts  6.33 us

profile of v1, /device:TPU:8, one launch (start us, length us, event | category | flops | bytes accessed | tf_op | source)
XLA Modules:
  0.0 219.4 jit_solution(3601593920118518524)
XLA Ops:
  0.6 95.6 %gather_all.1 = (bf16[2,4,64,8192]{3,2,1,0:T(8,128)(2,1)}, bf16[2,4,64,1024]{3,2,1,0:T(8,128)(2,1)}, bf16[2,4,64,1024]{3,2,1,0:T(8,128)(2,1)}, bf16[8,1024,256]{2,1,0:T(8,128)(2,1)}, bf16[8,1024,256]{2,1,0:T(8,128)(2,1)}) custom-call(bf16[2,64,8192]{2,1,0:T(8,128)(2,1)} %bitcast.24, bf16[2,64,4096]{2,1,0:T(8,128)(2,1)} %bitcast.25, ...), custom_call_target="tpu_custom_call" | custom-call | tf_op jit(solution)/shard_map/gather_all/pallas_call | solution.py:226
  96.3 0.0 copy-start
  96.3 0.0 copy-start.2
  96.3 7.8 %fusion.1.val_raw = f32[512,256]{1,0:T(8,128)} fusion(bf16[512,8192]{1,0:T(8,128)(2,1)} %bitcast.21, bf16[8192,256]{1,0:T(8,128)(2,1)} %bitcast.35), kind=kOutput, calls=%fused_computation.3 | convolution fusion | flops 2147483648 | bytes 13107200 | tf_op jit(solution)/shard_map/dot_general | solution.py:563
  104.1 0.0 copy-done
  104.1 0.5 copy-done.2
  104.6 3.1 %fusion.key_raw = f32[512,256]{1,0:T(8,128)} fusion(bf16[512,8192]{1,0:T(8,128)(2,1)S(1)} %bitcast.23, bf16[8192,256]{1,0:T(8,128)(2,1)S(1)} %bitcast.34), kind=kOutput, calls=%fused_computation.2 | convolution fusion | flops 2147483648 | bytes 13107200 | tf_op jit(solution)/shard_map/dot_general | solution.py:562
  107.7 15.6 %attention.1 = (bf16[512,1024]{1,0:T(8,128)(2,1)}, bf16[512,1024]{1,0:T(8,128)(2,1)}, bf16[2,256,512]{2,1,0:T(8,128)(2,1)}) custom-call(f32[512,256]{1,0:T(8,128)} %fusion.key_raw, f32[512,256]{1,0:T(8,128)} %fusion.1.val_raw, f32[512,128]{1,0:T(8,128)} %constant.8.clone.cos, f32[512,128]{1,0:T(8,128)} %constant.9.clone.sin, ...), custom_call_target="tpu_custom_call" | custom-call | tf_op jit(solution)/shard_map/attention/pallas_call | solution.py:323
  123.3 88.5 %reduce_all.1 = (bf16[2,64,4096]{2,1,0:T(8,128)(2,1)}, bf16[2,64,4096]{2,1,0:T(8,128)(2,1)}, f32[512,1024]{1,0:T(8,128)}) custom-call(bf16[512,8192]{1,0:T(8,128)(2,1)} %bitcast.22, bf16[512,512]{1,0:T(8,128)(2,1)} %bitcast.33, bf16[2,4,64,1024]{3,2,1,0:T(8,128)(2,1)} %bitcast.31, bf16[2,4,64,1024]{3,2,1,0:T(8,128)(2,1)} %bitcast.32), custom_call_target="tpu_custom_call" | custom-call | tf_op jit(solution)/shard_map/reduce_all/pallas_call | solution.py:523
  211.7 1.7 slice_bitcast_fusion
  213.5 0.0 copy-start.1
  213.5 1.3 copy.14
  214.8 1.3 copy.13
  216.1 2.3 %copy.17 = bf16[1,2,64,4096]{3,2,1,0:T(8,128)(2,1)} copy(bf16[1,2,64,4096]{3,2,1,0:T(8,128)(2,1)} %bitcast.28) | data formatting | bytes 2097152
  218.4 0.0 copy-done.1
  218.4 1.0 copy.18
Async XLA Ops:
  96.3 7.9 %copy-start = (bf16[2,4,64,8192]{3,2,1,0:T(8,128)(2,1)S(1)}, bf16[2,4,64,8192]{3,2,1,0:T(8,128)(2,1)}, u32[]{:S(2)}) copy-start(bf16[2,4,64,8192]{3,2,1,0:T(8,128)(2,1)} %get-tuple-element.15) | copy-start | bytes 25165828
  96.3 8.3 %copy-start.2 = (bf16[8,1024,256]{2,1,0:T(8,128)(2,1)S(1)}, bf16[8,1024,256]{2,1,0:T(8,128)(2,1)}, u32[]{:S(2)}) copy-start(bf16[8,1024,256]{2,1,0:T(8,128)(2,1)} %get-tuple-element.16) | copy-start | bytes 12582916
  213.5 4.9 %copy-start.1 = (bf16[2,64,4096]{2,1,0:T(8,128)(2,1)S(1)}, bf16[2,64,4096]{2,1,0:T(8,128)(2,1)}, u32[]{:S(2)}) copy-start(bf16[2,64,4096]{2,1,0:T(8,128)(2,1)} %get-tuple-element.24) | copy-start | bytes 3145732

commit v2 on v1

v2 whole, which is shorter than its diff:
```python
import functools
import math

import jax
import jax.numpy as jnp
import numpy as np
from jax import lax
from jax.experimental import pallas as pl
from jax.experimental.pallas import tpu as pltpu
from jax.sharding import PartitionSpec as P

HEAD_WIDTH = 128
ROPE_BASE = 500000.0
CORES = 2
MESH = pl.DeviceIdType.MESH
ANY = pl.BlockSpec(memory_space=pl.ANY)
VMEM = pl.BlockSpec(memory_space=pltpu.VMEM)
VMEM_LIMIT = 63 << 20


def grid_of(count):
    rows = 2 if count % 2 == 0 else 1
    return rows, count // rows


def place(n_seq, n_dp):
    dp, seq = lax.axis_index("dp"), lax.axis_index("seq")
    chips = n_dp // CORES
    chip, core = lax.div(dp, CORES), lax.rem(dp, CORES)
    rows, cols = grid_of(n_seq)
    row, col = lax.div(seq, cols), lax.rem(seq, cols)
    row_peers = [row * cols + lax.rem(col + d, cols) for d in range(1, cols)]
    col_peers = [lax.rem(row + d, rows) * cols + col for d in range(1, rows)]
    far_peers = [
        lax.rem(row + e, rows) * cols + lax.rem(col + d, cols)
        for e in range(1, rows)
        for d in range(1, cols)
    ]
    return dp, seq, chips, chip, core, row_peers, col_peers, far_peers


def greet(dp, seq, chips, chip, core, peers):
    barrier = pltpu.get_barrier_semaphore()
    ids = [(dp, p) for p in peers]
    ids.append((chip * CORES + 1 - core, seq))
    if chips > 1:
        for d in (1, chips - 1):
            ids.append((lax.rem(chip + d, chips) * CORES + core, seq))
    for device in ids:
        pl.semaphore_signal(barrier, inc=1, device_id=device, device_id_type=MESH)
    pl.semaphore_wait(barrier, len(ids))


def kernel(
    n_seq, n_dp, kv_heads, group, tile,
    hidden, queries, key_matrix, value_matrix, out_grad, cos, sin, cos_t, sin_t,
    attn_out, qgrad_out, key_grad, val_grad,
    hid, qry, grd, key_all, val_all, key_raw, val_raw, keys, vals, attn, qgrad, pre_t,
    key_acc, val_acc, acc, mate_out, mate_in, chain_out, down_in, up_in,
    load_sem, own_sem, store_sem, hid_send, hid_recv, qry_send, qry_recv, grd_send, grd_recv,
    up_send, down_send, mate_w_send, w_recv, a_send, a_recv, q_send, q_recv,
    mate_send, mate_recv, chain_send, down_recv, up_recv,
):
    f32, bf16 = jnp.float32, jnp.bfloat16
    dp, seq, chips, chip, core, row_peers, col_peers, far_peers = place(n_seq, n_dp)
    peers = row_peers + col_peers + far_peers
    above, below = dp + CORES, dp - CORES
    mate = chip * CORES + 1 - core
    has_above, has_below = chip < chips - 1, chip > 0
    wide = group * HEAD_WIDTH
    width = kv_heads * wide
    total = keys.shape[0]
    half = HEAD_WIDTH // 2
    block = total // 2

    def head_cols(target, kv):
        return pl.ds(pl.multiple_of(target * width + kv * wide, wide), wide)

    loads = [
        (hidden, hid.at[:, seq], load_sem.at[0]),
        (key_matrix, key_all.at[dp], load_sem.at[1]),
        (value_matrix, val_all.at[dp], load_sem.at[2]),
    ]
    own_loads = []
    for kv in range(kv_heads):
        own_loads.append((
            (queries.at[:, :, head_cols(seq, kv)], qry.at[kv, :, seq], own_sem.at[0, kv]),
            (out_grad.at[:, :, head_cols(seq, kv)], grd.at[kv, :, seq], own_sem.at[1, kv]),
        ))
    greet(dp, seq, chips, chip, core, peers)
    sends = []
    slots = iter(range(hid_send.shape[0]))

    def send_hidden(source, part, target, src):
        copy = pltpu.make_async_remote_copy(
            src_ref=src, dst_ref=hid.at[part, source],
            send_sem=hid_send.at[next(slots)], recv_sem=hid_recv.at[source, part],
            device_id=(dp, target), device_id_type=MESH,
        )
        copy.start()
        sends.append(copy)

    def wait_hidden(source, part):
        pltpu.make_async_remote_copy(
            src_ref=hid.at[part, source], dst_ref=hid.at[part, source],
            send_sem=hid_send.at[0], recv_sem=hid_recv.at[source, part],
            device_id=(dp, source), device_id_type=MESH,
        ).wait_recv()

    tables = (key_all, val_all)
    owns = (key_matrix, value_matrix)

    def weight_copy(kind, piece, target_dp, send_sem, own=False):
        return pltpu.make_async_remote_copy(
            src_ref=owns[kind] if own else tables[kind].at[piece],
            dst_ref=tables[kind].at[piece],
            send_sem=send_sem, recv_sem=w_recv.at[piece, kind],
            device_id=(target_dp, seq), device_id_type=MESH,
        )

    def go(cond, copy_of, wait=False):
        @pl.when(cond)
        def _():
            copy = copy_of()
            copy.wait_send() if wait else copy.start()

    for p in row_peers:
        send_hidden(seq, 0, p, hidden.at[0])
    for p in col_peers:
        send_hidden(seq, 1, p, hidden.at[1])
    for kind in range(2):
        go(has_above, lambda: weight_copy(kind, dp, above, up_send.at[0, kind], True))
        go(has_below, lambda: weight_copy(kind, dp, below, down_send.at[0, kind], True))
    for p in row_peers:
        send_hidden(seq, 1, p, hidden.at[1])
    for p in col_peers:
        send_hidden(seq, 0, p, hidden.at[0])
    for kind in range(2):
        weight_copy(kind, dp, mate, mate_w_send.at[dp, kind], True).start()
    for copy in loads + [c for pair in own_loads for c in pair]:
        pltpu.make_async_copy(*copy).start()

    def relay_weight(step, kind):
        low, high = dp - CORES * step, dp + CORES * step

        @pl.when(chip >= step)
        def _():
            weight_copy(kind, low, below, up_send.at[step, kind]).wait_recv()
            go(has_above, lambda: weight_copy(kind, low, above, up_send.at[step, kind]))
            weight_copy(kind, low, mate, mate_w_send.at[low, kind]).start()

        @pl.when(chip + step < chips)
        def _():
            weight_copy(kind, high, above, down_send.at[step, kind]).wait_recv()
            go(has_below, lambda: weight_copy(kind, high, below, down_send.at[step, kind]))
            weight_copy(kind, high, mate, mate_w_send.at[high, kind]).start()

    def relay_hidden():
        for p in row_peers:
            wait_hidden(p, 0)
            for q in col_peers:
                send_hidden(p, 0, q, hid.at[0, p])
        for p in col_peers:
            wait_hidden(p, 1)
            for q in row_peers:
                send_hidden(p, 1, q, hid.at[1, p])

    def exchange(kv, src, dst, send_sem, recv_sem):
        for i, p in enumerate(peers):
            copy = pltpu.make_async_remote_copy(
                src_ref=src.at[:, :, head_cols(p, kv)], dst_ref=dst.at[kv, :, seq],
                send_sem=send_sem.at[kv, i], recv_sem=recv_sem.at[kv, seq],
                device_id=(dp, p), device_id_type=MESH,
            )
            copy.start()
            sends.append(copy)

    def wait_exchange(kv, dst, send_sem, recv_sem):
        for p in peers:
            pltpu.make_async_remote_copy(
                src_ref=dst.at[kv, :, p], dst_ref=dst.at[kv, :, p],
                send_sem=send_sem.at[kv, 0], recv_sem=recv_sem.at[kv, p],
                device_id=(dp, p), device_id_type=MESH,
            ).wait_recv()

    if chips > 1:
        relay_weight(1, 0)
    relay_hidden()
    for kv in range(kv_heads):
        exchange(kv, queries, qry, qry_send, qry_recv)
        exchange(kv, out_grad, grd, grd_send, grd_recv)
    if chips > 1:
        relay_weight(1, 1)
    for step in range(2, chips):
        for kind in range(2):
            relay_weight(step, kind)
    for p in row_peers:
        wait_hidden(p, 1)
    for p in col_peers:
        wait_hidden(p, 0)
    for p in far_peers:
        wait_hidden(p, 0)
        wait_hidden(p, 1)
    for other in range(chips):
        for kind in range(2):
            piece = other * CORES + 1 - core
            weight_copy(kind, piece, mate, mate_w_send.at[piece, kind]).wait_recv()
    for copy in loads:
        pltpu.make_async_copy(*copy).wait()

    key_raw[...] = jnp.zeros_like(key_raw)
    val_raw[...] = jnp.zeros_like(val_raw)
    deep = key_all.shape[1]

    @pl.loop(0, n_dp)
    def _(d):
        cols = pl.ds(pl.multiple_of(d * deep, deep), deep)
        rows = hid[:, :, :, cols].reshape(total, deep)
        key_raw[...] += jnp.dot(rows, key_all[d], preferred_element_type=f32)
        val_raw[...] += jnp.dot(rows, val_all[d], preferred_element_type=f32)

    for kv in range(kv_heads):
        lanes = pl.ds(kv * HEAD_WIDTH, HEAD_WIDTH)
        raw = key_raw[:, lanes]
        swapped = jnp.concatenate([raw[:, half:], raw[:, :half]], axis=1)
        keys[:, lanes] = (raw * cos[...] + swapped * sin[...]).astype(bf16)
    vals[...] = val_raw[...].astype(bf16)

    scale = 1.0 / math.sqrt(HEAD_WIDTH)
    nt = (((1,), (1,)), ((), ()))
    tn = (((0,), (0,)), ((), ()))

    def attend(kv):
        lanes = pl.ds(kv * HEAD_WIDTH, HEAD_WIDTH)
        key_acc[...] = jnp.zeros_like(key_acc)
        val_acc[...] = jnp.zeros_like(val_acc)

        @pl.loop(0, group)
        def _(m):
            head = pl.ds(pl.multiple_of(m * HEAD_WIDTH, HEAD_WIDTH), HEAD_WIDTH)
            for b in range(2):
                span = (b + 1) * block
                q = qry[kv, b, :, :, head].reshape(block, HEAD_WIDTH)
                g = grd[kv, b, :, :, head].reshape(block, HEAD_WIDTH)
                k, v = keys[:span, lanes], vals[:span, lanes]
                s = lax.dot_general(q, k, nt, preferred_element_type=f32) * scale
                at = b * block + lax.broadcasted_iota(jnp.int32, s.shape, 0)
                col = lax.broadcasted_iota(jnp.int32, s.shape, 1)
                s = jnp.where(col <= at, s, -jnp.inf)
                e = jnp.exp(s - jnp.max(s, axis=1, keepdims=True))
                p = e * (1.0 / jnp.sum(e, axis=1, keepdims=True))
                p_half = p.astype(bf16)
                o = jnp.dot(p_half, v, preferred_element_type=f32).astype(bf16)
                attn[kv, b, :, :, head] = o.reshape(n_seq, block // n_seq, HEAD_WIDTH)
                dot = jnp.sum(g.astype(f32) * o.astype(f32), axis=1, keepdims=True)
                gp = lax.dot_general(g, v, nt, preferred_element_type=f32)
                ds = (p * (gp - dot) * scale).astype(bf16)
                dq = jnp.dot(ds, k, preferred_element_type=f32).astype(bf16)
                qgrad[kv, b, :, :, head] = dq.reshape(n_seq, block // n_seq, HEAD_WIDTH)
                key_acc[:, :span] += lax.dot_general(q, ds, tn, preferred_element_type=f32)
                val_acc[:, :span] += lax.dot_general(g, p_half, tn, preferred_element_type=f32)

        grown = key_acc[...]
        swapped = jnp.concatenate([grown[half:, :], grown[:half, :]], axis=0)
        pre_t[kv, :HEAD_WIDTH, :] = (grown * cos_t[...] - swapped * sin_t[...]).astype(bf16)
        pre_t[kv, HEAD_WIDTH:, :] = val_acc[...].astype(bf16)

    height, depth = acc.shape[2], acc.shape[3]
    results = ((attn, attn_out, a_send, a_recv), (qgrad, qgrad_out, q_send, q_recv))

    def own_store(kv, which):
        src, dst, _, _ = results[which]
        return pltpu.make_async_copy(
            src.at[kv, :, seq], dst.at[:, :, head_cols(seq, kv)], store_sem.at[which, kv]
        )

    def give_back(kv):
        for which, (src, dst, send_sem, recv_sem) in enumerate(results):
            for i, p in enumerate(peers):
                copy = pltpu.make_async_remote_copy(
                    src_ref=src.at[kv, :, p], dst_ref=dst.at[:, :, head_cols(seq, kv)],
                    send_sem=send_sem.at[kv, i], recv_sem=recv_sem.at[kv, seq],
                    device_id=(dp, p), device_id_type=MESH,
                )
                copy.start()
                sends.append(copy)
            own_store(kv, which).start()

    def wait_back(kv):
        for which, (src, dst, send_sem, recv_sem) in enumerate(results):
            for p in peers:
                pltpu.make_async_remote_copy(
                    src_ref=src.at[kv, :, p], dst_ref=dst.at[:, :, head_cols(p, kv)],
                    send_sem=send_sem.at[kv, 0], recv_sem=recv_sem.at[kv, p],
                    device_id=(dp, p), device_id_type=MESH,
                ).wait_recv()
            own_store(kv, which).wait()

    def mate_copy(kv, t):
        return pltpu.make_async_remote_copy(
            src_ref=mate_out.at[kv, t], dst_ref=mate_in.at[kv, t],
            send_sem=mate_send.at[kv, t], recv_sem=mate_recv.at[kv, t],
            device_id=(mate, seq), device_id_type=MESH,
        )

    def chain_copy(kv, t, down):
        return pltpu.make_async_remote_copy(
            src_ref=chain_out.at[kv, t], dst_ref=(down_in if down else up_in).at[kv, t],
            send_sem=chain_send.at[kv, t], recv_sem=(down_recv if down else up_recv).at[kv, t],
            device_id=(below if down else above, seq), device_id_type=MESH,
        )

    def product(kv, which, store):
        @pl.loop(0, depth // tile)
        def _(i):
            cols = pl.ds(pl.multiple_of(which * depth + i * tile, tile), tile)
            rows = hid[:, :, :, cols].reshape(total, tile)
            part = jnp.dot(pre_t[kv], rows, preferred_element_type=f32)
            store(pl.ds(pl.multiple_of(i * tile, tile), tile), part)

    def products(kv):
        @pl.loop(0, chips)
        def _(i):
            odd, k = lax.rem(i, 2), lax.div(i, 2)
            t = odd * (chips - 1 - k) + (1 - odd) * k

            def to_mate(cols, part):
                mate_out[kv, t, :, cols] = part.astype(bf16)

            def to_acc(cols, part):
                acc[kv, t, :, cols] = part

            product(kv, t * CORES + 1 - core, to_mate)
            mate_copy(kv, t).start()
            product(kv, t * CORES + core, to_acc)

    strip = 32

    def sweep(fn):
        @pl.loop(0, height // strip)
        def _(i):
            fn(pl.ds(pl.multiple_of(i * strip, strip), strip))

    def relay(kv, t, down, has_input):
        mate_copy(kv, t).wait_recv()

        def merge(extra):
            def fn(rows):
                v = acc[kv, t, rows, :]
                for e in (mate_in,) + extra:
                    v = v + e[kv, t, rows, :].astype(f32)
                chain_out[kv, t, rows, :] = v.astype(bf16)

            sweep(fn)

        @pl.when(has_input)
        def _():
            chain_copy(kv, t, down).wait_recv()
            merge((down_in if down else up_in,))

        @pl.when(jnp.logical_not(has_input))
        def _():
            merge(())

        chain_copy(kv, t, down).start()

    is_end = jnp.logical_or(chip == 0, chip == chips - 1)

    def chain(kv, cond):
        @pl.when(cond)
        def _():
            @pl.loop(0, chips - 1)
            def _(tau):
                k_down = tau - (chips - 1 - chip)
                k_up = tau - chip

                @pl.when(jnp.logical_and(k_down >= 0, k_down < chip))
                def _():
                    relay(kv, k_down, True, has_above)

                @pl.when(jnp.logical_and(k_up >= 0, k_up < chips - 1 - chip))
                def _():
                    relay(kv, chips - 1 - k_up, False, has_below)

    def finish(kv):
        mate_copy(kv, chip).wait_recv()

        def take(extra):
            def fn(rows):
                acc[kv, chip, rows, :] += extra[kv, chip, rows, :].astype(f32)

            sweep(fn)

        take(mate_in)

        @pl.when(has_above)
        def _():
            chain_copy(kv, chip, True).wait_recv()
            take(down_in)

        @pl.when(has_below)
        def _():
            chain_copy(kv, chip, False).wait_recv()
            take(up_in)

        lanes = pl.ds(kv * HEAD_WIDTH, HEAD_WIDTH)

        @pl.loop(0, depth // HEAD_WIDTH)
        def _(j):
            at = pl.ds(pl.multiple_of(j * HEAD_WIDTH, HEAD_WIDTH), HEAD_WIDTH)
            key_grad[at, lanes] = acc[kv, chip, :HEAD_WIDTH, at].T
            val_grad[at, lanes] = acc[kv, chip, HEAD_WIDTH:, at].T

    last = kv_heads - 1
    for kv in range(kv_heads):
        wait_exchange(kv, qry, qry_send, qry_recv)
        wait_exchange(kv, grd, grd_send, grd_recv)
        for copy in own_loads[kv]:
            pltpu.make_async_copy(*copy).wait()
        attend(kv)
        products(kv)
        give_back(kv)
        if kv < last:
            chain(kv, is_end)
    for kv in range(kv_heads):
        chain(kv, jnp.logical_not(is_end) if kv < last else chip >= 0)
    for kv in range(kv_heads):
        finish(kv)
    for kv in range(kv_heads):
        wait_back(kv)
    for copy in sends:
        copy.wait_send()
    for kind in range(2):
        for step in range(max(chips - 1, 1)):
            low, high = dp - CORES * step, dp + CORES * step
            go(jnp.logical_and(has_above, chip >= step),
               lambda: weight_copy(kind, low, above, up_send.at[step, kind]), True)
            go(jnp.logical_and(has_below, chip + step < chips),
               lambda: weight_copy(kind, high, below, down_send.at[step, kind]), True)
        for other in range(chips):
            piece = other * CORES + core
            weight_copy(kind, piece, mate, mate_w_send.at[piece, kind]).wait_send()
    for kv in range(kv_heads):
        for t in range(chips):
            mate_copy(kv, t).wait_send()
            go(chip != t, lambda: chain_copy(kv, t, True), True)


def local(n_seq, n_dp, hidden, queries, key_matrix, value_matrix, out_grad):
    _, stretches, tokens, embed = hidden.shape
    full = queries.shape[3]
    width = full // n_seq
    deep, kv_width = key_matrix.shape
    kv_heads = kv_width // HEAD_WIDTH
    group = width // kv_width
    wide = group * HEAD_WIDTH
    chips = n_dp // CORES
    rows, cols = grid_of(n_seq)
    hid_sends = 2 * (rows - 1 + cols - 1) + 2 * (rows - 1) * (cols - 1)
    total = stretches * n_seq * tokens
    bf16, f32 = jnp.bfloat16, jnp.float32
    dma = pltpu.SemaphoreType.DMA
    half = HEAD_WIDTH // 2
    inverse = np.exp(
        np.arange(half, dtype=np.float32) * np.float32(-2.0 * math.log(ROPE_BASE) / HEAD_WIDTH)
    ).astype(np.float32)
    phase = np.arange(total, dtype=np.float32)[:, None] * inverse[None, :]
    cos_half, sin_half = np.cos(phase), np.sin(phase)
    cos = np.concatenate([cos_half, cos_half], axis=1).astype(np.float32)
    sin = np.concatenate([-sin_half, sin_half], axis=1).astype(np.float32)
    heads = (kv_heads, stretches, n_seq, tokens, wide)
    height = 2 * HEAD_WIDTH
    blocks = (kv_heads, chips, height, deep)
    weights = (n_dp, deep, kv_width)
    attn_out, query_grad, key_grad, val_grad = pl.pallas_call(
        functools.partial(kernel, n_seq, n_dp, kv_heads, group, math.gcd(deep, 256)),
        out_shape=[
            jax.ShapeDtypeStruct((stretches, tokens, full), bf16),
            jax.ShapeDtypeStruct((stretches, tokens, full), bf16),
            jax.ShapeDtypeStruct((deep, kv_width), f32),
            jax.ShapeDtypeStruct((deep, kv_width), f32),
        ],
        in_specs=[ANY] * 5 + [VMEM] * 4,
        out_specs=[ANY, ANY, VMEM, VMEM],
        scratch_shapes=[
            pltpu.VMEM((stretches, n_seq, tokens, embed), bf16),
            pltpu.VMEM(heads, bf16),
            pltpu.VMEM(heads, bf16),
            pltpu.VMEM(weights, bf16),
            pltpu.VMEM(weights, bf16),
            pltpu.VMEM((total, kv_width), f32),
            pltpu.VMEM((total, kv_width), f32),
            pltpu.VMEM((total, kv_width), bf16),
            pltpu.VMEM((total, kv_width), bf16),
            pltpu.VMEM(heads, bf16),
            pltpu.VMEM(heads, bf16),
            pltpu.VMEM((kv_heads, height, total), bf16),
            pltpu.VMEM((HEAD_WIDTH, total), f32),
            pltpu.VMEM((HEAD_WIDTH, total), f32),
            pltpu.VMEM(blocks, f32),
            pltpu.VMEM(blocks, bf16),
            pltpu.VMEM(blocks, bf16),
            pltpu.VMEM(blocks, bf16),
            pltpu.VMEM(blocks, bf16),
            pltpu.VMEM(blocks, bf16),
            dma((3,)), dma((2, kv_heads)), dma((2, kv_heads)),
            dma((hid_sends,)), dma((n_seq, 2)),
            dma((kv_heads, n_seq)), dma((kv_heads, n_seq)),
            dma((kv_heads, n_seq)), dma((kv_heads, n_seq)),
            dma((chips, 2)), dma((chips, 2)), dma((n_dp, 2)), dma((n_dp, 2)),
            dma((kv_heads, n_seq)), dma((kv_heads, n_seq)),
            dma((kv_heads, n_seq)), dma((kv_heads, n_seq)),
            dma((kv_heads, chips)), dma((kv_heads, chips)), dma((kv_heads, chips)),
            dma((kv_heads, chips)), dma((kv_heads, chips)),
        ],
        compiler_params=pltpu.CompilerParams(
            collective_id=0, has_side_effects=True, vmem_limit_bytes=VMEM_LIMIT
        ),
        name="attention_step",
    )(hidden[0], queries[0], key_matrix, value_matrix, out_grad[0],
      cos, sin, cos.T.copy(), sin.T.copy())
    return attn_out[None], query_grad[None], key_grad, val_grad


def solution(mesh):
    n_dp, n_seq = mesh.shape["dp"], mesh.shape["seq"]
    tokens, weights = P("dp", None, "seq", None), P("dp", "seq")
    return jax.shard_map(
        functools.partial(local, n_seq, n_dp),
        mesh=mesh,
        in_specs=(tokens, tokens, weights, weights, tokens),
        out_specs=(tokens, tokens, weights, weights),
        check_vma=False,
    )
```

time: 220 us -> 178 us (0.81)
  Pallas kernels: 200 us -> 172 us
  matrix products: 11 us -> 0 us
  local copies, waits for them, and re-layouts: 8.06 us -> 5.36 us
    pallas_call x3 -> x1, Pallas kernels: 200 us -> 172 us  [local(): pl.pallas_call(functools.partial(kernel, n_seq, n_dp, kv_heads, group, ma...]
    dot_general x2 -> x0, matrix products: 11 us -> none  [the longest x1 7.85 us: local(): jnp.dot(hid, val_full.reshape(embed, kv_width), preferred_element_type=f32)]
where the time goes in v2:
time: 178 us
  Pallas kernels  172 us (97%)
  local copies, waits for them, and re-layouts  5.36 us (3%)
    pallas_call x1, Pallas kernels, local(): pl.pallas_call(functools.partial(kernel, n_seq, n_dp, kv_heads, group, ma...  172 us
    unnamed x10, local copies, waits for them, and re-layouts  5.36 us

profile of v2, /device:TPU:8, one launch (start us, length us, event | category | flops | bytes accessed | tf_op | source)
XLA Modules:
  0.0 178.3 jit_solution(11978217026813769308)
XLA Ops:
  0.6 172.3 %attention_step.1 = (bf16[2,64,4096]{2,1,0:T(8,128)(2,1)}, bf16[2,64,4096]{2,1,0:T(8,128)(2,1)}, f32[1024,256]{1,0:T(8,128)}, f32[1024,256]{1,0:T(8,128)}) custom-call(bf16[2,64,8192]{2,1,0:T(8,128)(2,1)} %bitcast.5, bf16[2,64,4096]{2,1,0:T(8,128)(2,1)} %bitcast.8, bf16[1024,256]{1,0:T(8,128)(2,1)} %key_matrix.1, bf16[1024,256]{1,0:T(8,128)(2,1)} %value_matrix.1, ...), custom_call_target="tpu_custom_call" | custom-call | tf_op jit(solution)/shard_map/attention_step/pallas_call | solution.py:475
  173.0 0.0 copy-start.2
  173.0 0.0 copy-start.1
  173.0 2.4 %copy.17 = bf16[1,2,64,4096]{3,2,1,0:T(8,128)(2,1)} copy(bf16[1,2,64,4096]{3,2,1,0:T(8,128)(2,1)} %bitcast.7) | data formatting | bytes 2097152
  175.4 0.0 copy-done.2
  175.4 0.0 copy-start
  175.4 1.0 copy.18
  176.4 0.0 copy-done.1
  176.4 1.0 copy.19
  177.4 0.0 copy-done
  177.4 1.0 copy.20
Async XLA Ops:
  173.0 2.5 %copy-start.2 = (bf16[2,64,4096]{2,1,0:T(8,128)(2,1)S(1)}, bf16[2,64,4096]{2,1,0:T(8,128)(2,1)}, u32[]{:S(2)}) copy-start(bf16[2,64,4096]{2,1,0:T(8,128)(2,1)} %get-tuple-element.9) | copy-start | bytes 3145732
  173.0 3.4 %copy-start.1 = (f32[1024,256]{1,0:T(8,128)S(1)}, f32[1024,256]{1,0:T(8,128)}, u32[]{:S(2)}) copy-start(f32[1024,256]{1,0:T(8,128)} %get-tuple-element.18) | copy-start | bytes 3145732
  175.4 1.9 %copy-start = (f32[1024,256]{1,0:T(8,128)S(1)}, f32[1024,256]{1,0:T(8,128)}, u32[]{:S(2)}) copy-start(f32[1024,256]{1,0:T(8,128)} %get-tuple-element.19) | copy-start | bytes 3145732

commit v3 on v2

--- a/solution.py
+++ b/solution.py
@@ -55,7 +55,7 @@
     n_seq, n_dp, kv_heads, group, tile,
     hidden, queries, key_matrix, value_matrix, out_grad, cos, sin, cos_t, sin_t,
     attn_out, qgrad_out, key_grad, val_grad,
-    hid, qry, grd, key_all, val_all, key_raw, val_raw, keys, vals, attn, qgrad, pre_t,
+    hid, qry, grd, key_all, val_all, raw_both, keys, vals, attn, qgrad, pre_t,
     key_acc, val_acc, acc, mate_out, mate_in, chain_out, down_in, up_in,
     load_sem, own_sem, store_sem, hid_send, hid_recv, qry_send, qry_recv, grd_send, grd_recv,
     up_send, down_send, mate_w_send, w_recv, a_send, a_recv, q_send, q_recv,
@@ -76,17 +76,22 @@
     def head_cols(target, kv):
         return pl.ds(pl.multiple_of(target * width + kv * wide, wide), wide)
 
+    def one_head(target, h):
+        start = pl.multiple_of(target * width + h * HEAD_WIDTH, HEAD_WIDTH)
+        return pl.ds(start, HEAD_WIDTH)
+
     loads = [
         (hidden, hid.at[:, seq], load_sem.at[0]),
         (key_matrix, key_all.at[dp], load_sem.at[1]),
         (value_matrix, val_all.at[dp], load_sem.at[2]),
     ]
-    own_loads = []
-    for kv in range(kv_heads):
-        own_loads.append((
-            (queries.at[:, :, head_cols(seq, kv)], qry.at[kv, :, seq], own_sem.at[0, kv]),
-            (out_grad.at[:, :, head_cols(seq, kv)], grd.at[kv, :, seq], own_sem.at[1, kv]),
-        ))
+
+    def own_loads(h):
+        return (
+            (queries.at[:, :, one_head(seq, h)], qry.at[h, :, seq], own_sem.at[0, h]),
+            (out_grad.at[:, :, one_head(seq, h)], grd.at[h, :, seq], own_sem.at[1, h]),
+        )
+
     greet(dp, seq, chips, chip, core, peers)
     sends = []
     slots = iter(range(hid_send.shape[0]))
@@ -137,7 +142,7 @@
         send_hidden(seq, 0, p, hidden.at[0])
     for kind in range(2):
         weight_copy(kind, dp, mate, mate_w_send.at[dp, kind], True).start()
-    for copy in loads + [c for pair in own_loads for c in pair]:
+    for copy in loads + [c for h in range(kv_heads * group) for c in own_loads(h)]:
         pltpu.make_async_copy(*copy).start()
 
     def relay_weight(step, kind):
@@ -165,30 +170,30 @@
             for q in row_peers:
                 send_hidden(p, 1, q, hid.at[1, p])
 
-    def exchange(kv, src, dst, send_sem, recv_sem):
+    def exchange(h, src, dst, send_sem, recv_sem):
         for i, p in enumerate(peers):
             copy = pltpu.make_async_remote_copy(
-                src_ref=src.at[:, :, head_cols(p, kv)], dst_ref=dst.at[kv, :, seq],
-                send_sem=send_sem.at[kv, i], recv_sem=recv_sem.at[kv, seq],
+                src_ref=src.at[:, :, one_head(p, h)], dst_ref=dst.at[h, :, seq],
+                send_sem=send_sem.at[h, i], recv_sem=recv_sem.at[h, seq],
                 device_id=(dp, p), device_id_type=MESH,
             )
             copy.start()
             sends.append(copy)
 
-    def wait_exchange(kv, dst, send_sem, recv_sem):
+    def wait_exchange(h, dst, send_sem, recv_sem):
         for p in peers:
             pltpu.make_async_remote_copy(
-                src_ref=dst.at[kv, :, p], dst_ref=dst.at[kv, :, p],
-                send_sem=send_sem.at[kv, 0], recv_sem=recv_sem.at[kv, p],
+                src_ref=dst.at[h, :, p], dst_ref=dst.at[h, :, p],
+                send_sem=send_sem.at[h, 0], recv_sem=recv_sem.at[h, p],
                 device_id=(dp, p), device_id_type=MESH,
             ).wait_recv()
 
     if chips > 1:
         relay_weight(1, 0)
     relay_hidden()
-    for kv in range(kv_heads):
-        exchange(kv, queries, qry, qry_send, qry_recv)
-        exchange(kv, out_grad, grd, grd_send, grd_recv)
+    for h in range(kv_heads * group):
+        exchange(h, queries, qry, qry_send, qry_recv)
+        exchange(h, out_grad, grd, grd_send, grd_recv)
     if chips > 1:
         relay_weight(1, 1)
     for step in range(2, chips):
@@ -208,23 +213,23 @@
     for copy in loads:
         pltpu.make_async_copy(*copy).wait()
 
-    key_raw[...] = jnp.zeros_like(key_raw)
-    val_raw[...] = jnp.zeros_like(val_raw)
     deep = key_all.shape[1]
 
-    @pl.loop(0, n_dp)
-    def _(d):
-        cols = pl.ds(pl.multiple_of(d * deep, deep), deep)
-        rows = hid[:, :, :, cols].reshape(total, deep)
-        key_raw[...] += jnp.dot(rows, key_all[d], preferred_element_type=f32)
-        val_raw[...] += jnp.dot(rows, val_all[d], preferred_element_type=f32)
-
-    for kv in range(kv_heads):
+    def project(kv):
         lanes = pl.ds(kv * HEAD_WIDTH, HEAD_WIDTH)
-        raw = key_raw[:, lanes]
+        raw_both[...] = jnp.zeros_like(raw_both)
+
+        @pl.loop(0, n_dp)
+        def _(d):
+            cols = pl.ds(pl.multiple_of(d * deep, deep), deep)
+            rows = hid[:, :, :, cols].reshape(total, deep)
+            both = jnp.concatenate([key_all[d, :, lanes], val_all[d, :, lanes]], axis=1)
+            raw_both[...] += jnp.dot(rows, both, preferred_element_type=f32)
+
+        raw = raw_both[:, :HEAD_WIDTH]
         swapped = jnp.concatenate([raw[:, half:], raw[:, :half]], axis=1)
         keys[:, lanes] = (raw * cos[...] + swapped * sin[...]).astype(bf16)
-    vals[...] = val_raw[...].astype(bf16)
+        vals[:, lanes] = raw_both[:, HEAD_WIDTH:].astype(bf16)
 
     scale = 1.0 / math.sqrt(HEAD_WIDTH)
     nt = (((1,), (1,)), ((), ()))
@@ -238,10 +243,15 @@
         @pl.loop(0, group)
         def _(m):
             head = pl.ds(pl.multiple_of(m * HEAD_WIDTH, HEAD_WIDTH), HEAD_WIDTH)
+            h = kv * group + m
+            wait_exchange(h, qry, qry_send, qry_recv)
+            wait_exchange(h, grd, grd_send, grd_recv)
+            for copy in own_loads(h):
+                pltpu.make_async_copy(*copy).wait()
             for b in range(2):
                 span = (b + 1) * block
-                q = qry[kv, b, :, :, head].reshape(block, HEAD_WIDTH)
-                g = grd[kv, b, :, :, head].reshape(block, HEAD_WIDTH)
+                q = qry[h, b].reshape(block, HEAD_WIDTH)
+                g = grd[h, b].reshape(block, HEAD_WIDTH)
                 k, v = keys[:span, lanes], vals[:span, lanes]
                 s = lax.dot_general(q, k, nt, preferred_element_type=f32) * scale
                 at = b * block + lax.broadcasted_iota(jnp.int32, s.shape, 0)
@@ -318,22 +328,6 @@
             part = jnp.dot(pre_t[kv], rows, preferred_element_type=f32)
             store(pl.ds(pl.multiple_of(i * tile, tile), tile), part)
 
-    def products(kv):
-        @pl.loop(0, chips)
-        def _(i):
-            odd, k = lax.rem(i, 2), lax.div(i, 2)
-            t = odd * (chips - 1 - k) + (1 - odd) * k
-
-            def to_mate(cols, part):
-                mate_out[kv, t, :, cols] = part.astype(bf16)
-
-            def to_acc(cols, part):
-                acc[kv, t, :, cols] = part
-
-            product(kv, t * CORES + 1 - core, to_mate)
-            mate_copy(kv, t).start()
-            product(kv, t * CORES + core, to_acc)
-
     strip = 32
 
     def sweep(fn):
@@ -353,18 +347,51 @@
 
             sweep(fn)
 
-        @pl.when(has_input)
-        def _():
+        if has_input:
             chain_copy(kv, t, down).wait_recv()
             merge((down_in if down else up_in,))
-
-        @pl.when(jnp.logical_not(has_input))
-        def _():
+        else:
             merge(())
-
         chain_copy(kv, t, down).start()
 
     is_end = jnp.logical_or(chip == 0, chip == chips - 1)
+
+    flip = lax.div(chips - 1 - chip, max(chips - 1, 1)) if chips > 1 else 0
+
+    def turn(i):
+        odd, k = lax.rem(i, 2), lax.div(i, 2)
+        t = odd * (chips - 1 - k) + (1 - odd) * k
+        return flip * (chips - 1 - t) + (1 - flip) * t
+
+    def early(kv, t):
+        @pl.when(jnp.logical_and(chip == chips - 1, t < chip))
+        def _():
+            relay(kv, t, True, False)
+
+        @pl.when(jnp.logical_and(chip == 0, t > chip))
+        def _():
+            relay(kv, t, False, False)
+
+    def products(kv):
+        @pl.loop(0, chips)
+        def _(i):
+            t = turn(i)
+
+            def to_mate(cols, part):
+                mate_out[kv, t, :, cols] = part.astype(bf16)
+
+            def to_acc(cols, part):
+                acc[kv, t, :, cols] = part
+
+            product(kv, t * CORES + 1 - core, to_mate)
+            mate_copy(kv, t).start()
+            product(kv, t * CORES + core, to_acc)
+
+            @pl.when(i > 0)
+            def _():
+                early(kv, turn(i - 1))
+
+        early(kv, turn(chips - 1))
 
     def chain(kv, cond):
         @pl.when(cond)
@@ -376,58 +403,68 @@
 
                 @pl.when(jnp.logical_and(k_down >= 0, k_down < chip))
                 def _():
-                    relay(kv, k_down, True, has_above)
+                    relay(kv, k_down, True, True)
 
                 @pl.when(jnp.logical_and(k_up >= 0, k_up < chips - 1 - chip))
                 def _():
-                    relay(kv, chips - 1 - k_up, False, has_below)
+                    relay(kv, chips - 1 - k_up, False, True)
+
+    def prepare(kv):
+        mate_copy(kv, chip).wait_recv()
+
+        def fn(rows):
+            acc[kv, chip, rows, :] += mate_in[kv, chip, rows, :].astype(f32)
+
+        sweep(fn)
 
     def finish(kv):
-        mate_copy(kv, chip).wait_recv()
-
-        def take(extra):
-            def fn(rows):
-                acc[kv, chip, rows, :] += extra[kv, chip, rows, :].astype(f32)
-
-            sweep(fn)
-
-        take(mate_in)
+        lanes = pl.ds(kv * HEAD_WIDTH, HEAD_WIDTH)
+
+        def put(extra):
+            @pl.loop(0, depth // HEAD_WIDTH)
+            def _(j):
+                at = pl.ds(pl.multiple_of(j * HEAD_WIDTH, HEAD_WIDTH), HEAD_WIDTH)
+                v = acc[kv, chip, :, at]
+                for e in extra:
+                    v = v + e[kv, chip, :, at].astype(f32)
+                key_grad[at, lanes] = v[:HEAD_WIDTH, :].T
+                val_grad[at, lanes] = v[HEAD_WIDTH:, :].T
+
+        if chips == 1:
+            put(())
+            return
 
         @pl.when(has_above)
         def _():
             chain_copy(kv, chip, True).wait_recv()
-            take(down_in)
 
         @pl.when(has_below)
         def _():
             chain_copy(kv, chip, False).wait_recv()
-            take(up_in)
-
-        lanes = pl.ds(kv * HEAD_WIDTH, HEAD_WIDTH)
-
-        @pl.loop(0, depth // HEAD_WIDTH)
-        def _(j):
-            at = pl.ds(pl.multiple_of(j * HEAD_WIDTH, HEAD_WIDTH), HEAD_WIDTH)
-            key_grad[at, lanes] = acc[kv, chip, :HEAD_WIDTH, at].T
-            val_grad[at, lanes] = acc[kv, chip, HEAD_WIDTH:, at].T
-
-    last = kv_heads - 1
+
+        @pl.when(chip == 0)
+        def _():
+            put((down_in,))
+
+        @pl.when(chip == chips - 1)
+        def _():
+            put((up_in,))
+
+        @pl.when(jnp.logical_not(is_end))
+        def _():
+            put((down_in, up_in))
+
     for kv in range(kv_heads):
-        wait_exchange(kv, qry, qry_send, qry_recv)
-        wait_exchange(kv, grd, grd_send, grd_recv)
-        for copy in own_loads[kv]:
-            pltpu.make_async_copy(*copy).wait()
+        project(kv)
         attend(kv)
         products(kv)
         give_back(kv)
-        if kv < last:
-            chain(kv, is_end)
     for kv in range(kv_heads):
-        chain(kv, jnp.logical_not(is_end) if kv < last else chip >= 0)
-    for kv in range(kv_heads):
-        finish(kv)
+        prepare(kv)
+        chain(kv, jnp.logical_not(is_end))
     for kv in range(kv_heads):
         wait_back(kv)
+        finish(kv)
     for copy in sends:
         copy.wait_send()
     for kind in range(2):
@@ -469,6 +506,7 @@
     cos = np.concatenate([cos_half, cos_half], axis=1).astype(np.float32)
     sin = np.concatenate([-sin_half, sin_half], axis=1).astype(np.float32)
     heads = (kv_heads, stretches, n_seq, tokens, wide)
+    single = (kv_heads * group, stretches, n_seq, tokens, HEAD_WIDTH)
     height = 2 * HEAD_WIDTH
     blocks = (kv_heads, chips, height, deep)
     weights = (n_dp, deep, kv_width)
@@ -484,12 +522,11 @@
         out_specs=[ANY, ANY, VMEM, VMEM],
         scratch_shapes=[
             pltpu.VMEM((stretches, n_seq, tokens, embed), bf16),
-            pltpu.VMEM(heads, bf16),
-            pltpu.VMEM(heads, bf16),
+            pltpu.VMEM(single, bf16),
+            pltpu.VMEM(single, bf16),
             pltpu.VMEM(weights, bf16),
             pltpu.VMEM(weights, bf16),
-            pltpu.VMEM((total, kv_width), f32),
-            pltpu.VMEM((total, kv_width), f32),
+            pltpu.VMEM((total, 2 * HEAD_WIDTH), f32),
             pltpu.VMEM((total, kv_width), bf16),
             pltpu.VMEM((total, kv_width), bf16),
             pltpu.VMEM(heads, bf16),
@@ -503,10 +540,10 @@
             pltpu.VMEM(blocks, bf16),
             pltpu.VMEM(blocks, bf16),
             pltpu.VMEM(blocks, bf16),
-            dma((3,)), dma((2, kv_heads)), dma((2, kv_heads)),
+            dma((3,)), dma((2, kv_heads * group)), dma((2, kv_heads)),
             dma((hid_sends,)), dma((n_seq, 2)),
-            dma((kv_heads, n_seq)), dma((kv_heads, n_seq)),
-            dma((kv_heads, n_seq)), dma((kv_heads, n_seq)),
+            dma((kv_heads * group, n_seq)), dma((kv_heads * group, n_seq)),
+            dma((kv_heads * group, n_seq)), dma((kv_heads * group, n_seq)),
             dma((chips, 2)), dma((chips, 2)), dma((n_dp, 2)), dma((n_dp, 2)),
             dma((kv_heads, n_seq)), dma((kv_heads, n_seq)),
             dma((kv_heads, n_seq)), dma((kv_heads, n_seq)),

time: 178 us -> 172 us (0.966)
  Pallas kernels: 172 us -> 166 us
    pallas_call x1, Pallas kernels: 172 us -> 166 us  [local(): pl.pallas_call(functools.partial(kernel, n_seq, n_dp, kv_heads, group, ma...]
where the time goes in v3:
time: 172 us
  Pallas kernels  166 us (97%)
  local copies, waits for them, and re-layouts  5.36 us (3%)
    pallas_call x1, Pallas kernels, local(): pl.pallas_call(functools.partial(kernel, n_seq, n_dp, kv_heads, group, ma...  166 us
    unnamed x10, local copies, waits for them, and re-layouts  5.36 us

profile of v3, /device:TPU:8, one launch (start us, length us, event | category | flops | bytes accessed | tf_op | source)
XLA Modules:
  0.0 171.9 jit_solution(3465282589596206539)
XLA Ops:
  0.6 165.9 %attention_step.1 = (bf16[2,64,4096]{2,1,0:T(8,128)(2,1)}, bf16[2,64,4096]{2,1,0:T(8,128)(2,1)}, f32[1024,256]{1,0:T(8,128)}, f32[1024,256]{1,0:T(8,128)}) custom-call(bf16[2,64,8192]{2,1,0:T(8,128)(2,1)} %bitcast.5, bf16[2,64,4096]{2,1,0:T(8,128)(2,1)} %bitcast.8, bf16[1024,256]{1,0:T(8,128)(2,1)} %key_matrix.1, bf16[1024,256]{1,0:T(8,128)(2,1)} %value_matrix.1, ...), custom_call_target="tpu_custom_call" | custom-call | tf_op jit(solution)/shard_map/attention_step/pallas_call | solution.py:513
  166.6 0.0 copy-start.2
  166.6 0.0 copy-start.1
  166.6 2.4 %copy.17 = bf16[1,2,64,4096]{3,2,1,0:T(8,128)(2,1)} copy(bf16[1,2,64,4096]{3,2,1,0:T(8,128)(2,1)} %bitcast.7) | data formatting | bytes 2097152
  169.0 0.0 copy-done.2
  169.0 0.0 copy-start
  169.0 1.0 copy.18
  170.0 0.0 copy-done.1
  170.0 1.0 copy.19
  171.0 0.0 copy-done
  171.0 1.0 copy.20
Async XLA Ops:
  166.6 2.5 %copy-start.2 = (bf16[2,64,4096]{2,1,0:T(8,128)(2,1)S(1)}, bf16[2,64,4096]{2,1,0:T(8,128)(2,1)}, u32[]{:S(2)}) copy-start(bf16[2,64,4096]{2,1,0:T(8,128)(2,1)} %get-tuple-element.9) | copy-start | bytes 3145732
  166.6 3.4 %copy-start.1 = (f32[1024,256]{1,0:T(8,128)S(1)}, f32[1024,256]{1,0:T(8,128)}, u32[]{:S(2)}) copy-start(f32[1024,256]{1,0:T(8,128)} %get-tuple-element.18) | copy-start | bytes 3145732
  169.0 1.9 %copy-start = (f32[1024,256]{1,0:T(8,128)S(1)}, f32[1024,256]{1,0:T(8,128)}, u32[]{:S(2)}) copy-start(f32[1024,256]{1,0:T(8,128)} %get-tuple-element.19) | copy-start | bytes 3145732

commit v4 on v3

--- a/solution.py
+++ b/solution.py
@@ -15,7 +15,7 @@
 MESH = pl.DeviceIdType.MESH
 ANY = pl.BlockSpec(memory_space=pl.ANY)
 VMEM = pl.BlockSpec(memory_space=pltpu.VMEM)
-VMEM_LIMIT = 63 << 20
+VMEM_LIMIT = 56 << 20
 
 
 def grid_of(count):
@@ -513,13 +513,13 @@
     attn_out, query_grad, key_grad, val_grad = pl.pallas_call(
         functools.partial(kernel, n_seq, n_dp, kv_heads, group, math.gcd(deep, 256)),
         out_shape=[
-            jax.ShapeDtypeStruct((stretches, tokens, full), bf16),
-            jax.ShapeDtypeStruct((stretches, tokens, full), bf16),
-            jax.ShapeDtypeStruct((deep, kv_width), f32),
-            jax.ShapeDtypeStruct((deep, kv_width), f32),
+            pltpu.VMEM((stretches, tokens, full), bf16),
+            pltpu.VMEM((stretches, tokens, full), bf16),
+            pltpu.VMEM((deep, kv_width), f32),
+            pltpu.VMEM((deep, kv_width), f32),
         ],
         in_specs=[ANY] * 5 + [VMEM] * 4,
-        out_specs=[ANY, ANY, VMEM, VMEM],
+        out_specs=[VMEM] * 4,
         scratch_shapes=[
             pltpu.VMEM((stretches, n_seq, tokens, embed), bf16),
             pltpu.VMEM(single, bf16),

time: 172 us -> 169 us (0.983)
    unnamed x10 -> x4, local copies, waits for them, and re-layouts: 5.36 us -> 3.88 us
where the time goes in v4:
time: 169 us
  Pallas kernels  165 us (98%)
  local copies, waits for them, and re-layouts  3.88 us (2%)
    pallas_call x1, Pallas kernels, local(): pl.pallas_call(functools.partial(kernel, n_seq, n_dp, kv_heads, group, ma...  165 us
    unnamed x4, local copies, waits for them, and re-layouts  3.88 us

profile of v4, /device:TPU:8, one launch (start us, length us, event | category | flops | bytes accessed | tf_op | source)
XLA Modules:
  0.0 169.1 jit_solution(2007628764771707550)
XLA Ops:
  0.6 164.6 %attention_step.1 = (bf16[2,64,4096]{2,1,0:T(8,128)(2,1)S(1)}, bf16[2,64,4096]{2,1,0:T(8,128)(2,1)S(1)}, f32[1024,256]{1,0:T(8,128)S(1)}, f32[1024,256]{1,0:T(8,128)S(1)}) custom-call(bf16[2,64,8192]{2,1,0:T(8,128)(2,1)} %bitcast.7, bf16[2,64,4096]{2,1,0:T(8,128)(2,1)} %bitcast.8, bf16[1024,256]{1,0:T(8,128)(2,1)} %key_matrix.1, ...), custom_call_target="tpu_custom_call" | custom-call | tf_op jit(solution)/shard_map/attention_step/pallas_call | solution.py:513
  165.2 1.0 copy.17
  166.2 1.0 copy.18
  167.2 1.0 copy.19
  168.2 1.0 copy.20

commit v5 on v4

--- a/solution.py
+++ b/solution.py
@@ -481,6 +481,30 @@
         for t in range(chips):
             mate_copy(kv, t).wait_send()
             go(chip != t, lambda: chain_copy(kv, t, True), True)
+
+
+def put_kernel(*refs):
+    count = len(refs) // 2
+    sem = refs[-1]
+    copies = [
+        pltpu.make_async_copy(refs[i], refs[count + i], sem.at[i]) for i in range(count)
+    ]
+    for copy in copies:
+        copy.start()
+    for copy in copies:
+        copy.wait()
+
+
+def put_all(*arrays):
+    return pl.pallas_call(
+        put_kernel,
+        out_shape=[jax.ShapeDtypeStruct(x.shape, x.dtype) for x in arrays],
+        in_specs=[pl.BlockSpec(memory_space=pltpu.VMEM)] * len(arrays),
+        out_specs=[ANY] * len(arrays),
+        scratch_shapes=[pltpu.SemaphoreType.DMA((len(arrays),))],
+        compiler_params=pltpu.CompilerParams(vmem_limit_bytes=1 << 20),
+        name="put_all",
+    )(*arrays)
 
 
 def local(n_seq, n_dp, hidden, queries, key_matrix, value_matrix, out_grad):
@@ -556,6 +580,9 @@
         name="attention_step",
     )(hidden[0], queries[0], key_matrix, value_matrix, out_grad[0],
       cos, sin, cos.T.copy(), sin.T.copy())
+    attn_out, query_grad, key_grad, val_grad = put_all(
+        attn_out, query_grad, key_grad, val_grad
+    )
     return attn_out[None], query_grad[None], key_grad, val_grad
 
 

time: 169 us -> 167 us (0.988)
  local copies, waits for them, and re-layouts: 3.88 us -> 0 us
  Pallas kernels: 165 us -> 167 us
    unnamed x4 -> x0, local copies, waits for them, and re-layouts: 3.88 us -> none
    pallas_call x0 -> x1, Pallas kernels: none -> 2.04 us  [put_all(): pl.pallas_call(put_kernel, out_shape=[jax.ShapeDtypeStruct(x.shape, x.dty...]
where the time goes in v5:
time: 167 us
  Pallas kernels  167 us (100%)
    pallas_call x1, Pallas kernels, local(): pl.pallas_call(functools.partial(kernel, n_seq, n_dp, kv_heads, group, ma...  165 us

profile of v5, /device:TPU:8, one launch (start us, length us, event | category | flops | bytes accessed | tf_op | source)
XLA Modules:
  0.0 167.3 jit_solution(13400961125249923602)
XLA Ops:
  0.6 164.6 %attention_step.1 = (bf16[2,64,4096]{2,1,0:T(8,128)(2,1)S(1)}, bf16[2,64,4096]{2,1,0:T(8,128)(2,1)S(1)}, f32[1024,256]{1,0:T(8,128)S(1)}, f32[1024,256]{1,0:T(8,128)S(1)}) custom-call(bf16[2,64,8192]{2,1,0:T(8,128)(2,1)} %bitcast.5, bf16[2,64,4096]{2,1,0:T(8,128)(2,1)} %bitcast.6, bf16[1024,256]{1,0:T(8,128)(2,1)} %key_matrix.1, ...), custom_call_target="tpu_custom_call" | custom-call | tf_op jit(solution)/shard_map/attention_step/pallas_call | solution.py:537
  165.2 2.0 %put_all.1 = (bf16[2,64,4096]{2,1,0:T(8,128)(2,1)}, bf16[2,64,4096]{2,1,0:T(8,128)(2,1)}, f32[1024,256]{1,0:T(8,128)}, f32[1024,256]{1,0:T(8,128)}) custom-call(bf16[2,64,4096]{2,1,0:T(8,128)(2,1)S(1)} %get-tuple-element.12.refs_0_, bf16[2,64,4096]{2,1,0:T(8,128)(2,1)S(1)} %get-tuple-element.13.refs_1_, f32[1024,256]{1,0:T(8,128)S(1)} %get-tuple-element.14.refs_2_, ...), custom_call_target="tpu_custom_call" | custom-call | tf_op jit(solution)/shard_map/put_all/pallas_call | solution.py:499
